TPU v7x, 32 devices: a whole 2x2x4 slice. The times are simulated.
32 devices in a mesh: space: 4 (over y, core), energy: 8 (over z, x).
Axes of the slice: x: 2, y: 2, z: 4, core: 2. Of those that a mesh axis runs over, the one named last changes fastest.
Arguments:
- ham_diag: float32 [8, 2, 128, 128], P('space'), may hold values from -0.5 to 0.5
- coupling: float32 [8, 2, 128, 128], P('space'), may hold values from -0.5 to 0.5
- contact_left: float32 [2, 128, 128], replicated, may hold values from -0.5 to 0.5
- mode_weight: float32 [4], replicated, may hold values from 0.5 to 2
- mode_offset: int32 [4], replicated, may hold values from -4 to 4, as said below
- pattern: int32 [128, 128], replicated, may hold values 0 or 1
Outputs:
- sigma: float32 [8, 8, 2, 128, 128], P('energy', 'space')
Inputs may be any that keep to these rules, and one draw needn't show every extreme that they name: `mode_offset`: the offsets are -1, 1, -4 and 4 in some order.
All inputs are finite; a program needn't handle non-finite values.
Results may differ from a plain program's by a relative error of at most 0.0003.
Values sent between devices are 32-bit elements; how exact they have to be, the bound alone decides.
No kernel may reach another device: no remote copies, remote signals or barrier semaphores. Data moves between devices by JAX's collectives and lax.ppermute only.
A program may use at most 64 MiB of HBM per device.

v0:
```python
import functools
import math

import jax
import jax.numpy as jnp
from jax import lax
from jax.experimental import pallas as pl
from jax.experimental.pallas import tpu as pltpu
from jax.sharding import PartitionSpec as P

HIGHEST = lax.Precision.HIGHEST
BROADENING = 0.1
F32 = jnp.float32
BF16 = jnp.bfloat16


FULL_STEPS = 2
LOW_STEPS = 2
MOST_STEPS = 20
SETTLED = 0.999
RESIDUE_LIMIT = 4e-3
SAFE_STEPS = 64
KERNEL_VMEM = 24 << 20


def dot(a, b):
    return jnp.dot(a, b, preferred_element_type=F32)


def operand(b):
    n = b.shape[1] // 2
    return jnp.concatenate([b, jnp.concatenate([-b[:, n:], b[:, :n]], 1)], 0)


def halves(a):
    high = a.astype(BF16)
    return high, (a - high.astype(F32)).astype(BF16)


def mul_full(a, b):
    return jnp.dot(a, operand(b), precision=HIGHEST, preferred_element_type=F32)


def mul_split(a, b):
    a_high, a_low = halves(a)
    b_high, b_low = halves(b)
    b_high, b_low = operand(b_high), operand(b_low)
    return dot(a_high, b_high) + (dot(a_high, b_low) + dot(a_low, b_high))


def mul_low(a, b):
    return dot(a.astype(BF16), operand(b.astype(BF16)))


mul = mul_full


def adj(a):
    n = a.shape[1] // 2
    return jnp.concatenate([a[:, :n].T, -a[:, n:].T], 1)


def unit(n):
    row = lax.broadcasted_iota(jnp.int32, (n, 2 * n), 0)
    col = lax.broadcasted_iota(jnp.int32, (n, 2 * n), 1)
    return (row == col).astype(F32)


def times_half_imag(a):
    n = a.shape[1] // 2
    return jnp.concatenate([-0.5 * a[:, n:], 0.5 * a[:, :n]], 1)


def total(a):
    return jnp.sum(jnp.sum(a, axis=0, keepdims=True), axis=1, keepdims=True)


def start(a):
    back = adj(a)
    normal = mul_full(a, back)
    scale = 1.0 / jnp.sqrt(total(normal * normal))
    return back, normal, scale


def thresholds():
    value = SETTLED
    for _ in range(MOST_STEPS):
        yield value
        value = value / (2.0 - value + 2.0 * math.sqrt(1.0 - value))


def invert_fast(mats):
    n = mats[0].shape[0]
    one = unit(n)
    state = []
    lowest = None
    for a in mats:
        back, normal, scale = start(a)
        least = (0.99 * BROADENING**2) * scale
        lowest = least if lowest is None else jnp.minimum(lowest, least)
        state.append((back, one - normal * scale, least, scale))
    lowest = lowest[0, 0]
    count = jnp.int32(0)
    for value in thresholds():
        count = count + (lowest < value).astype(jnp.int32)

    def step(multiply, _, state):
        fresh = []
        for x, rest, least, gain in state:
            c = 2.0 / (1.0 + least)
            centred = (1.0 - c) * one + c * rest
            both = multiply(jnp.concatenate([x, centred], 0), centred)
            fresh.append((x + both[:n], both[n:], jnp.minimum(c * c * least, 1.0), c * gain))
        return tuple(fresh)

    state = tuple(state)
    for k in range(FULL_STEPS):
        state = step(mul_full, k, state)
    middle = jnp.maximum(count - (FULL_STEPS + LOW_STEPS), 0)
    state = lax.fori_loop(0, middle, functools.partial(step, mul_split), state)
    state = lax.fori_loop(0, LOW_STEPS, functools.partial(step, mul_low), state)
    found, worst = [], jnp.zeros((1, 1), F32)
    for a, (x, _, _, gain) in zip(mats, state):
        x = x * gain
        residue = one - mul_full(a, x)
        worst = jnp.maximum(worst, total(residue * residue))
        found.append(x + mul_split(x, residue))
    return found, worst


def invert_safe(mats):
    n = mats[0].shape[0]
    one = unit(n)
    found = []
    for a in mats:
        back, _, scale = start(a)

        def step(_, x):
            return x + mul_full(x, one - mul_full(a, x))

        x = lax.fori_loop(0, SAFE_STEPS, step, back * scale)
        found.append(x)
    return found, jnp.zeros((1, 1), F32)


def row_form(ref, index=None):
    if index is None:
        return jnp.concatenate([ref[0], ref[1]], 1)
    return jnp.concatenate([ref[index, 0], ref[index, 1]], 1)


def place():
    position = lax.axis_index("space")
    chip = position // 2
    core = position % 2
    right = (chip >= lax.axis_size("space") // 4).astype(jnp.int32)
    outer = (core == right).astype(jnp.int32)
    return position, core, right, outer


def load(pairs, sems):
    copies = [pltpu.make_async_copy(src, dst, sems.at[k]) for k, (src, dst) in enumerate(pairs)]
    for copy in copies:
        copy.start()
    return copies


def prepared(ham, cpl):
    n = ham.shape[-1]
    _, core, _, _ = place()
    energy_count = lax.axis_size("energy")
    rank = lax.axis_index("energy")
    near = rank + 1 - 2 * (rank % 2)
    solved = jnp.where(core == 0, near, (rank + energy_count // 2) % energy_count)
    energy = -2.0 + (solved.astype(F32) + 0.5) * (4.0 / energy_count)
    one = unit(n)
    shift = energy * one + BROADENING * jnp.concatenate([one[:, n:], one[:, :n]], 1)
    hams = [row_form(ham, k) for k in range(2)]
    links = [row_form(cpl, k) for k in range(2)]
    return [shift - 0.5 * (m + adj(m)) for m in hams], links, [adj(m) for m in links]


BACK, CONTACT, LINKS = 4, 8, 10


def block_index(k):
    _, _, right, outer = place()
    return (2 * (1 - outer) if k < 2 else 2 * outer) + (k % 2 + right * (1 - 2 * (k % 2)))


def chip_index(j, core):
    return (2 * core if j < 2 else 2 * (1 - core)) + j % 2


def link_index(k):
    _, core, right, _ = place()
    at = jnp.where(right == 1, chip_index(2 - k, core), chip_index(k, core))
    return at + BACK * right, at + BACK * (1 - right)


def fill(ham, cpl, base, blocks_ref, links_ref):
    blocks, links, backs = prepared(ham, cpl)
    for k in range(2):
        blocks_ref[base + k] = blocks[k]
        links_ref[base + k] = links[k]
        links_ref[BACK + base + k] = backs[k]


def own_kernel(ham_hbm, cpl_hbm, contact_hbm, blocks_ref, links_ref, ham, cpl, contact, sems):
    for copy in load([(ham_hbm, ham), (cpl_hbm, cpl), (contact_hbm, contact)], sems):
        copy.wait()
    fill(ham, cpl, 0, blocks_ref, links_ref)
    lead = row_form(contact)
    links_ref[CONTACT] = lead
    links_ref[CONTACT + 1] = adj(lead)


def join_kernel(own_blocks, own_links, ham, cpl, blocks_ref, links_ref, head_ref, last_ref):
    _, core, right, _ = place()
    fill(ham, cpl, 2, blocks_ref, links_ref)
    end = chip_index(3, core)
    lead = links_ref[jnp.where(right == 1, BACK + end, CONTACT)]
    lead_back = links_ref[jnp.where(right == 1, end, CONTACT + 1)]
    last_ref[...] = links_ref[end]
    head_ref[...] = times_half_imag(mul(lead, lead_back))


B0, B1, B2, T0, P1, P2, Q, R, RECORD = range(9)


def chain_links(turned):
    found = [link_index(k) for k in range(3)]
    if turned:
        found = [(b, a) for a, b in found[::-1]]
    return [a for a, _ in found] + [b for _, b in found]


def eliminate(blocks, links, head, record, schur_ref, corner_ref, invert):
    c0, c1, c2, c0h, c1h, c2h = links
    (b0, b2), bad = invert([blocks[0] + head, blocks[2]])
    t0 = mul(b0, c0)
    p1 = mul(b2, c1h)
    p2 = mul(b2, c2)
    record[B0], record[B2], record[T0], record[P1], record[P2] = b0, b2, t0, p1, p2
    middle = blocks[1] - mul(c0h, t0) - mul(c1, p1)
    upper = mul(c1, p2)
    lower = mul(c2h, p1)
    tail = blocks[3] - mul(c2h, p2)
    (b1,), more = invert([middle])
    bad = jnp.maximum(bad, more)
    q = mul(b1, upper)
    r = mul(lower, b1)
    schur = tail - mul(lower, q)
    record[B1], record[Q], record[R] = b1, q, r
    schur_ref[...] = schur
    (corner,), more = invert([schur])
    corner_ref[...] = corner
    return jnp.maximum(bad, more)


def chip_ends(links_ref, before_ref):
    _, core, right, _ = place()
    ahead = before_ref[...]
    back = adj(ahead)
    end = chip_index(3, core)
    last, last_back = links_ref[end], links_ref[BACK + end]
    mirrored = right == 1
    pick = lambda a, b: jnp.where(mirrored, a, b)
    return [pick(last, back), pick(last_back, ahead), pick(back, last), pick(ahead, last_back)]


def ends_kernel(links_ref, before_ref, out_ref):
    for k, value in enumerate(chip_ends(links_ref, before_ref)):
        out_ref[k] = value


def head_kernel(link_ref, back_ref, message_ref, out_ref):
    out_ref[...] = -mul(mul(link_ref[...], message_ref[...]), back_ref[...])


def eliminate_kernel(turned, blocks_ref, links_ref, head_ref, record_ref, schur_ref, corner_ref):
    def run(invert):
        return eliminate(
            [blocks_ref[block_index(3 - k if turned else k)] for k in range(4)],
            [links_ref[at] for at in chain_links(turned)],
            head_ref[...],
            record_ref,
            schur_ref,
            corner_ref,
            invert,
        )

    bad = jnp.sum(run(invert_fast))

    @pl.when(jnp.logical_not(bad < RESIDUE_LIMIT))
    def _():
        run(invert_safe)


def spread_kernel(links_ref, record_ref, before_ref, out_ref):
    c0, c1, _, c0h, _, c2h = (links_ref[at] for at in chain_links(False))
    b0, b1, b2, t0, p1, p2, q, r = (record_ref[k] for k in range(RECORD))
    w0 = mul(c0h, b0)
    m1 = mul(c1, b2)
    m2 = mul(c2h, b2)
    out_ref[0] = b0 + mul(mul(t0, b1), w0)
    out_ref[1] = b1
    out_ref[2] = b2 + mul(mul(p1, b1), m1)
    out_ref[3] = mul(t0, q)
    out_ref[4] = q
    out_ref[5] = mul(p1, q) + p2
    out_ref[6] = mul(r, w0)
    out_ref[7] = r
    out_ref[8] = mul(r, m1) + m2
    _, _, out_ref[9], out_ref[10] = chip_ends(links_ref, before_ref)


def finish_kernel(schur_ref, spread_ref, message_ref, mine_ref, theirs_ref):
    _, core, right, outer = place()
    n = schur_ref.shape[0]

    def run(invert):
        closed = schur_ref[...] - mul(mul(spread_ref[9], message_ref[...]), spread_ref[10])
        (full,), bad = invert([closed])
        reach = mul(jnp.concatenate([spread_ref[3 + j] for j in range(3)], 0), full)
        green = [spread_ref[j] + mul(reach[j * n : (j + 1) * n], spread_ref[6 + j]) for j in range(3)] + [full]

        def store(outer_ref, inner_ref):
            for k in range(4):
                ref = outer_ref if k < 2 else inner_ref
                index = jnp.where(right == 1, 1 - k % 2, k % 2)
                ref[index, 0] = green[k][:, :n]
                ref[index, 1] = green[k][:, n:]

        @pl.when(outer == 1)
        def _():
            store(mine_ref, theirs_ref)

        @pl.when(outer == 0)
        def _():
            store(theirs_ref, mine_ref)

        return bad

    bad = jnp.sum(run(invert_fast))

    @pl.when(jnp.logical_not(bad < RESIDUE_LIMIT))
    def _():
        run(invert_safe)


def combine_kernel(
    weight_ref, offset_ref, mine_ref, partner_ref, third_a, third_b, pattern_hbm, out_ref, pattern_ref, sem
):
    _, core, _, _ = place()
    pltpu.sync_copy(pattern_hbm, pattern_ref)
    energy_count = lax.axis_size("energy")
    rank = lax.axis_index("energy")
    half = energy_count // 2
    near = rank + 1 - 2 * (rank % 2)
    away = 2 * rank - near
    far = (rank + half) % energy_count

    def weight_of(source):
        found = jnp.float32(0.0)
        for m in range(weight_ref.shape[0]):
            found = found + jnp.where(offset_ref[m] == rank - source, weight_ref[m], 0.0)
        return found

    near_weight = weight_of(near)
    far_weight = weight_of(far)
    away_weight = weight_of(away)
    mine_weight = jnp.where(core == 0, near_weight, far_weight)
    partner_weight = jnp.where(core == 0, far_weight, near_weight)
    keep = pattern_ref[...].astype(F32)
    for k in range(out_ref.shape[1]):
        for part in range(2):
            value = mine_weight * mine_ref[k, part] + partner_weight * partner_ref[k, part]
            value = value + away_weight * jnp.where(core == 0, third_a[k, part], third_b[k, part])
            out_ref[0, k, part] = value * keep


def kernel(body, shapes, where, scratch=(), aliases=None, result="v"):
    spaces = {"s": pltpu.SMEM, "v": pltpu.VMEM, "a": pl.ANY}
    many = len(shapes) > 1
    if result == "v":
        outs = [pltpu.VMEM(shape, F32) for shape in shapes]
    else:
        outs = [jax.ShapeDtypeStruct(shape, F32) for shape in shapes]
    out_specs = [pl.BlockSpec(memory_space=pltpu.VMEM) for _ in shapes]
    call = pl.pallas_call(
        body,
        out_shape=outs if many else outs[0],
        in_specs=[pl.BlockSpec(memory_space=spaces[w]) for w in where],
        out_specs=out_specs if many else out_specs[0],
        scratch_shapes=list(scratch),
        input_output_aliases=aliases or {},
        compiler_params=pltpu.CompilerParams(vmem_limit_bytes=KERNEL_VMEM),
    )

    def placed(*operands):
        return call(*(
            pltpu.with_memory_space_constraint(x, pltpu.VMEM) if w == "v" else x for x, w in zip(operands, where)
        ))

    return placed


def on_device(ham_diag, coupling, contact_left, mode_weight, mode_offset, pattern):
    n = ham_diag.shape[-1]
    assert ham_diag.shape[0] == 2
    space = lax.axis_size("space")
    energies = lax.axis_size("energy")
    chips = space // 2
    middle = chips // 2
    assert chips % 2 == 0 and space % 2 == 0 and energies % 4 == 0
    position = lax.axis_index("space")
    chip = position // 2
    depth = jnp.where(chip < middle, chip, chips - 1 - chip)
    swap = [(p, p ^ 1) for p in range(space)]

    row = (n, 2 * n)
    pair = (2, 2, n, n)
    vmem = lambda *shape: pltpu.VMEM(shape, F32)
    sems = lambda count: pltpu.SemaphoreType.DMA((count,))

    ham_far = lax.ppermute(ham_diag, "space", swap)
    cpl_far = lax.ppermute(coupling, "space", swap)

    own = kernel(
        own_kernel, [(4,) + row, (LINKS,) + row], "aaa", [vmem(*pair), vmem(*pair), vmem(2, n, n), sems(3)]
    )(ham_diag, coupling, contact_left)
    blocks, links, head, last = kernel(
        join_kernel, [(4,) + row, (LINKS,) + row, row, row], "vvvv", aliases={0: 0, 1: 1}
    )(*own, ham_far, cpl_far)
    forward, backward = (
        kernel(functools.partial(eliminate_kernel, turned), [(RECORD,) + row, row, row], "vvv")
        for turned in (False, True)
    )
    def chip_move(value, pairs):
        return lax.ppermute(value, "space", [(2 * a + k, 2 * b + k) for a, b in pairs for k in range(2)])

    before = chip_move(last, [(c, c + 1) for c in range(chips - 1)])
    state = forward(blocks, links, head)

    if middle > 1:
        ends = kernel(ends_kernel, [(4,) + row], "vv")(links, before)
        head_of = kernel(head_kernel, [row], "vvv")
    for d in range(1, middle):
        inward = [(c, c + 1) for c in range(middle - 1)] + [(c + 1, c) for c in range(middle, chips - 1)]
        fresh = forward(blocks, links, head_of(ends[0], ends[1], chip_move(state[2], inward)))
        state = [jnp.where(depth >= d, a, b) for a, b in zip(fresh, state)]
    record, schur, corner = state

    message = chip_move(corner, [(middle - 1, middle), (middle, middle - 1)])
    spread = kernel(spread_kernel, [(11,) + row], "vvv")(links, record, before)
    for d in range(middle - 2, -1, -1):
        outward = [(c + 1, c) for c in range(middle - 1)] + [(c, c + 1) for c in range(middle, chips - 1)]
        fresh = backward(blocks, links, head_of(ends[2], ends[3], message))
        message = jnp.where(depth == d, chip_move(fresh[2], outward), message)

    mine, theirs = kernel(finish_kernel, [pair, pair], "vvv")(schur, spread, message)
    partner = lax.ppermute(theirs, "space", swap)

    def flat(p, e):
        return p * energies + e

    hops = [(e - 2, e) for e in range(2, energies, 2)] + [(e + 2, e) for e in range(1, energies - 2, 2)]
    third = [
        lax.ppermute(
            mine if k == 0 else theirs,
            ("space", "energy"),
            [(flat(2 * c, a), flat(2 * c + k, b)) for c in range(chips) for a, b in hops],
        )
        for k in range(2)
    ]
    return kernel(
        combine_kernel, [(1,) + pair], "ssvvvva", [pltpu.VMEM(pattern.shape, jnp.int32), sems(1)], result="a"
    )(mode_weight, mode_offset, mine, partner, third[0], third[1], pattern)


def solution(mesh):
    placed = (P("space", None, None, None), P("space", None, None, None), P(), P(), P(), P())
    return jax.shard_map(
        on_device,
        mesh=mesh,
        in_specs=placed,
        out_specs=P("energy", "space", None, None, None),
        check_vma=False,
    )
```

profile of v0, /device:TPU:0, one launch (start us, length us, event | category | flops | bytes accessed | tf_op | source)
XLA Modules:
  0.0 49.9 jit_solution(13450317592662424108)
XLA Ops:
  0.0 0.5 collective-permute-start
  0.5 0.0 collective-permute-start.1
  0.5 0.0 copy-start
  0.5 0.9 %copy-done = f32[2,2,128,128]{3,2,1,0:T(8,128)S(1)} copy-done((f32[2,2,128,128]{3,2,1,0:T(8,128)S(1)}, f32[2,2,128,128]{3,2,1,0:T(8,128)}, u32[]{:S(2)}) %copy-start) | copy-done | bytes 262168
  1.5 0.0 copy-start.1
  1.5 0.9 %copy-done.1 = f32[2,2,128,128]{3,2,1,0:T(8,128)S(1)} copy-done((f32[2,2,128,128]{3,2,1,0:T(8,128)S(1)}, f32[2,2,128,128]{3,2,1,0:T(8,128)}, u32[]{:S(2)}) %copy-start.1) | copy-done | bytes 262168
  2.4 0.0 copy-start.2
  2.4 0.9 %copy-done.2 = f32[2,128,128]{2,1,0:T(8,128)S(1)} copy-done((f32[2,128,128]{2,1,0:T(8,128)S(1)}, f32[2,128,128]{2,1,0:T(8,128)}, u32[]{:S(2)}) %copy-start.2) | copy-done | bytes 131096
  3.3 0.5 shard_map.64
  3.8 0.0 collective-permute-done.ham
  3.8 0.0 collective-permute-done.1.cpl
  3.8 0.4 shard_map.65
  4.2 4.9 %collective-permute-start.2 = (f32[128,256]{1,0:T(8,128)S(1)}, f32[128,256]{1,0:T(8,128)S(1)}, u32[]{:S(2)}, u32[]{:S(2)}) collective-permute-start(f32[128,256]{1,0:T(8,128)S(1)} %get-tuple-element.23), channel_id=1, source_target_pairs={{0,16},{8,24},{1,17},{9,25},{2,18},{10,26},{3,19},{11,27},{4,20},{... | collective-permute-start | bytes 393224 | tf_op jit(solution)/shard_map/ppermute | solution.py:441
  9.1 17.0 %shard_map.66 = (f32[8,128,256]{2,1,0:T(8,128)S(1)}, f32[128,256]{1,0:T(8,128)S(1)}, f32[128,256]{1,0:T(8,128)S(1)}) custom-call(f32[4,128,256]{2,1,0:T(8,128)S(1)} %get-tuple-element.18.blocks_ref, f32[10,128,256]{2,1,0:T(8,128)S(1)} %get-tuple-element.19.links_ref, f32[128,256]{1,0:T(8,128)S(1)} %get-tuple-element.20.head_ref), custom_call_target="tpu_custom_call" | custom-call | tf_op jit(solution)/shard_map/pallas_call | solution.py:402
  26.1 0.1 collective-permute-start.3
  26.2 0.0 collective-permute-done.2.before_ref
  26.2 1.6 %shard_map.67.spread_ref = f32[11,128,256]{2,1,0:T(8,128)S(1)} custom-call(f32[10,128,256]{2,1,0:T(8,128)S(1)} %get-tuple-element.19.links_ref, f32[8,128,256]{2,1,0:T(8,128)S(1)} %get-tuple-element.22.record_ref, f32[128,256]{1,0:T(8,128)S(1)} %collective-permute-done.2.before_ref), custom_call_target="tpu_custom_call" | custom-call | tf_op jit(solution)/shard_map/pallas_call | solution.py:402
  27.9 0.0 copy-start.3
  27.9 0.0 copy-start.4
  27.9 0.0 copy-start.5
  27.9 3.4 %collective-permute-done.3.message_ref = f32[128,256]{1,0:T(8,128)S(1)} collective-permute-done((f32[128,256]{1,0:T(8,128)S(1)}, f32[128,256]{1,0:T(8,128)S(1)}, u32[]{:S(2)}, u32[]{:S(2)}) %collective-permute-start.3) | collective-permute-done | bytes 131104 | tf_op jit(solution)/shard_map/ppermute | solution.py:441
  31.3 6.7 %shard_map.68 = (f32[2,2,128,128]{3,2,1,0:T(8,128)S(1)}, f32[2,2,128,128]{3,2,1,0:T(8,128)S(1)}) custom-call(f32[128,256]{1,0:T(8,128)S(1)} %get-tuple-element.21.schur_ref, f32[11,128,256]{2,1,0:T(8,128)S(1)} %shard_map.67.spread_ref, f32[128,256]{1,0:T(8,128)S(1)} %collective-permute-done.3.message_ref), custom_call_target="tpu_custom_call" | custom-call | tf_op jit(solution)/shard_map/pallas_call | solution.py:402
  38.0 3.6 %collective-permute-start.5 = (f32[2,2,128,128]{3,2,1,0:T(8,128)S(1)}, f32[2,2,128,128]{3,2,1,0:T(8,128)S(1)}, u32[]{:S(2)}, u32[]{:S(2)}) collective-permute-start(f32[2,2,128,128]{3,2,1,0:T(8,128)S(1)} %get-tuple-element.25.mine_ref), channel_id=1, source_target_pairs={{0,2},{2,4},{4,6},{3,1},{5,3},{7,5},{16,18},{18,20},{20,22},{19,17... | collective-permute-start | bytes 786440 | tf_op jit(solution)/shard_map/ppermute | solution.py:470
  41.6 1.3 %collective-permute-start.6 = (f32[2,2,128,128]{3,2,1,0:T(8,128)S(1)}, f32[2,2,128,128]{3,2,1,0:T(8,128)S(1)}, u32[]{:S(2)}, u32[]{:S(2)}) collective-permute-start(f32[2,2,128,128]{3,2,1,0:T(8,128)S(1)} %get-tuple-element.26), channel_id=1, source_target_pairs={{0,10},{2,12},{4,14},{3,9},{5,11},{7,13},{16,26},{18,28},{20,30},{... | collective-permute-start | bytes 786440 | tf_op jit(solution)/shard_map/ppermute | solution.py:470
  42.9 0.1 collective-permute-start.4
  43.0 2.5 %collective-permute-done.5.third_a = f32[2,2,128,128]{3,2,1,0:T(8,128)S(1)} collective-permute-done((f32[2,2,128,128]{3,2,1,0:T(8,128)S(1)}, f32[2,2,128,128]{3,2,1,0:T(8,128)S(1)}, u32[]{:S(2)}, u32[]{:S(2)}) %collective-permute-start.5) | collective-permute-done | bytes 262176 | tf_op jit(solution)/shard_map/ppermute | solution.py:470
  45.5 2.8 %collective-permute-done.6.third_b = f32[2,2,128,128]{3,2,1,0:T(8,128)S(1)} collective-permute-done((f32[2,2,128,128]{3,2,1,0:T(8,128)S(1)}, f32[2,2,128,128]{3,2,1,0:T(8,128)S(1)}, u32[]{:S(2)}, u32[]{:S(2)}) %collective-permute-start.6) | collective-permute-done | bytes 262176 | tf_op jit(solution)/shard_map/ppermute | solution.py:470
  48.3 0.0 collective-permute-done.4.partner_ref
  48.3 0.0 copy-done.3
  48.3 0.0 copy-done.4
  48.3 0.0 copy-done.5
  48.3 1.5 %shard_map.69 = f32[1,2,2,128,128]{4,3,2,1,0:T(8,128)} custom-call(f32[4]{0:T(128)S(1)} %copy-done.4, s32[4]{0:T(128)S(1)} %copy-done.5, f32[2,2,128,128]{3,2,1,0:T(8,128)S(1)} %get-tuple-element.25.mine_ref, f32[2,2,128,128]{3,2,1,0:T(8,128)S(1)} %collective-permute-done.4.partner_ref, f32[2,2,128,128]{3,2,1,0:T(8,128)S(1)} %collective-permute-done.5.third_a, ...), custom_call_target="tpu_custom_call" | custom-call | tf_op jit(solution)/shard_map/pallas_call | solution.py:402
Async XLA Ops:
  0.0 3.8 %collective-permute-start = (f32[2,2,128,128]{3,2,1,0:T(8,128)}, f32[2,2,128,128]{3,2,1,0:T(8,128)S(1)}, u32[]{:S(2)}, u32[]{:S(2)}) collective-permute-start(f32[2,2,128,128]{3,2,1,0:T(8,128)} %ham_hbm.1), channel_id=1, source_target_pairs={{0,8},{8,0},{16,24},{24,16},{1,9},{9,1},{17,25},{25,17},{2,10},{10... | collective-permute-start | bytes 786440 | tf_op jit(solution)/shard_map/ppermute | solution.py:427
  0.5 3.3 %collective-permute-start.1 = (f32[2,2,128,128]{3,2,1,0:T(8,128)}, f32[2,2,128,128]{3,2,1,0:T(8,128)S(1)}, u32[]{:S(2)}, u32[]{:S(2)}) collective-permute-start(f32[2,2,128,128]{3,2,1,0:T(8,128)} %cpl_hbm.1), channel_id=1, source_target_pairs={{0,8},{8,0},{16,24},{24,16},{1,9},{9,1},{17,25},{25,17},{2,10},{10... | collective-permute-start | bytes 786440 | tf_op jit(solution)/shard_map/ppermute | solution.py:428
  0.5 0.9 %copy-start = (f32[2,2,128,128]{3,2,1,0:T(8,128)S(1)}, f32[2,2,128,128]{3,2,1,0:T(8,128)}, u32[]{:S(2)}) copy-start(f32[2,2,128,128]{3,2,1,0:T(8,128)} %ham_hbm.1) | copy-start | bytes 786436
  1.5 0.9 %copy-start.1 = (f32[2,2,128,128]{3,2,1,0:T(8,128)S(1)}, f32[2,2,128,128]{3,2,1,0:T(8,128)}, u32[]{:S(2)}) copy-start(f32[2,2,128,128]{3,2,1,0:T(8,128)} %cpl_hbm.1) | copy-start | bytes 786436
  2.4 0.9 %copy-start.2 = (f32[2,128,128]{2,1,0:T(8,128)S(1)}, f32[2,128,128]{2,1,0:T(8,128)}, u32[]{:S(2)}) copy-start(f32[2,128,128]{2,1,0:T(8,128)} %contact_hbm.1) | copy-start | bytes 393220
  4.2 22.0 %collective-permute-start.2 = (f32[128,256]{1,0:T(8,128)S(1)}, f32[128,256]{1,0:T(8,128)S(1)}, u32[]{:S(2)}, u32[]{:S(2)}) collective-permute-start(f32[128,256]{1,0:T(8,128)S(1)} %get-tuple-element.23), channel_id=1, source_target_pairs={{0,16},{8,24},{1,17},{9,25},{2,18},{10,26},{3,19},{11,27},{4,20},{... | collective-permute-start | bytes 393224 | tf_op jit(solution)/shard_map/ppermute | solution.py:441
  26.1 5.2 %collective-permute-start.3 = (f32[128,256]{1,0:T(8,128)S(1)}, f32[128,256]{1,0:T(8,128)S(1)}, u32[]{:S(2)}, u32[]{:S(2)}) collective-permute-start(f32[128,256]{1,0:T(8,128)S(1)} %get-tuple-element.24), channel_id=1, source_target_pairs={{0,16},{8,24},{16,0},{24,8},{1,17},{9,25},{17,1},{25,9},{2,18},{10... | collective-permute-start | bytes 393224 | tf_op jit(solution)/shard_map/ppermute | solution.py:441
  27.9 20.4 %copy-start.3 = (s32[128,128]{1,0:T(8,128)S(1)}, s32[128,128]{1,0:T(8,128)}, u32[]{:S(2)}) copy-start(s32[128,128]{1,0:T(8,128)} %pattern_hbm.1) | copy-start | bytes 196612
  27.9 20.4 %copy-start.4 = (f32[4]{0:T(128)S(1)}, f32[4]{0:T(128)}, u32[]{:S(2)}) copy-start(f32[4]{0:T(128)} %weight_ref.1) | copy-start | bytes 52
  27.9 20.4 %copy-start.5 = (s32[4]{0:T(128)S(1)}, s32[4]{0:T(128)}, u32[]{:S(2)}) copy-start(s32[4]{0:T(128)} %offset_ref.1) | copy-start | bytes 52
  38.0 7.4 %collective-permute-start.5 = (f32[2,2,128,128]{3,2,1,0:T(8,128)S(1)}, f32[2,2,128,128]{3,2,1,0:T(8,128)S(1)}, u32[]{:S(2)}, u32[]{:S(2)}) collective-permute-start(f32[2,2,128,128]{3,2,1,0:T(8,128)S(1)} %get-tuple-element.25.mine_ref), channel_id=1, source_target_pairs={{0,2},{2,4},{4,6},{3,1},{5,3},{7,5},{16,18},{18,20},{20,22},{19,17... | collective-permute-start | bytes 786440 | tf_op jit(solution)/shard_map/ppermute | solution.py:470
  41.6 6.7 %collective-permute-start.6 = (f32[2,2,128,128]{3,2,1,0:T(8,128)S(1)}, f32[2,2,128,128]{3,2,1,0:T(8,128)S(1)}, u32[]{:S(2)}, u32[]{:S(2)}) collective-permute-start(f32[2,2,128,128]{3,2,1,0:T(8,128)S(1)} %get-tuple-element.26), channel_id=1, source_target_pairs={{0,10},{2,12},{4,14},{3,9},{5,11},{7,13},{16,26},{18,28},{20,30},{... | collective-permute-start | bytes 786440 | tf_op jit(solution)/shard_map/ppermute | solution.py:470
  42.9 5.4 %collective-permute-start.4 = (f32[2,2,128,128]{3,2,1,0:T(8,128)S(1)}, f32[2,2,128,128]{3,2,1,0:T(8,128)S(1)}, u32[]{:S(2)}, u32[]{:S(2)}) collective-permute-start(f32[2,2,128,128]{3,2,1,0:T(8,128)S(1)} %get-tuple-element.26), channel_id=1, source_target_pairs={{0,8},{8,0},{16,24},{24,16},{1,9},{9,1},{17,25},{25,17},{2,10},{10... | collective-permute-start | bytes 786440 | tf_op jit(solution)/shard_map/ppermute | solution.py:463
where the time goes:
time: 50.2 us; the launch traced here: 49.9 us
  Pallas kernels  27.7 us (55%)
  starting transfers between devices  10.4 us (21%)
  waiting for transfers between devices  8.67 us (17%)
  local copies, waits for them, and re-layouts  2.82 us (6%)
    pallas_call x6, Pallas kernels, placed(): call(*(pltpu.with_memory_space_constraint(x, pltpu.VMEM) if w == 'v' else...  27.7 us
    ppermute x2, waiting for transfers between devices, on_device(): lax.ppermute(mine if k == 0 else theirs, ('space', 'energy'), [(flat(2 *...  5.27 us
    ppermute x2, starting transfers between devices, chip_move(): lax.ppermute(value, 'space', [(2 * a + k, 2 * b + k) for a, b in pairs fo...  4.98 us
    ppermute x2, starting transfers between devices, on_device(): lax.ppermute(mine if k == 0 else theirs, ('space', 'energy'), [(flat(2 *...  4.86 us
    ppermute x2, waiting for transfers between devices, chip_move(): lax.ppermute(value, 'space', [(2 * a + k, 2 * b + k) for a, b in pairs fo...  3.39 us
    unnamed x12, local copies, waits for them, and re-layouts  2.82 us
  transfers between devices with their start and end apart: 7, of which 3 were waited for; matrix products, arithmetic and copies ran while one was open for 0% of the time, Pallas kernels for 38%

commit v1 on v0

--- a/solution.py
+++ b/solution.py
@@ -8,14 +8,14 @@
 from jax.experimental.pallas import tpu as pltpu
 from jax.sharding import PartitionSpec as P
 
+
 HIGHEST = lax.Precision.HIGHEST
 BROADENING = 0.1
 F32 = jnp.float32
 BF16 = jnp.bfloat16
 
 
-FULL_STEPS = 2
-LOW_STEPS = 2
+LATE_STEPS = 2
 MOST_STEPS = 20
 SETTLED = 0.999
 RESIDUE_LIMIT = 4e-3
@@ -89,36 +89,44 @@
         value = value / (2.0 - value + 2.0 * math.sqrt(1.0 - value))
 
 
+def early_step(_, state):
+    fresh = []
+    for x, d, least, gain in state:
+        n = d.shape[0]
+        c = 2.0 / (1.0 + least)
+        both = mul_split(jnp.concatenate([d, x], 0), d)
+        fresh.append((2.0 * x - c * both[n:], c * (2.0 * d - c * both[:n]), jnp.minimum(c * c * least, 1.0), c * gain))
+    return tuple(fresh)
+
+
+def late_step(state):
+    fresh = []
+    for x, rest, least, gain in state:
+        n = rest.shape[0]
+        c = 2.0 / (1.0 + least)
+        centred = (1.0 - c) * unit(n) + c * rest
+        both = mul_low(jnp.concatenate([centred, x], 0), centred)
+        fresh.append((x + both[n:], both[:n], jnp.minimum(c * c * least, 1.0), c * gain))
+    return tuple(fresh)
+
+
 def invert_fast(mats):
-    n = mats[0].shape[0]
-    one = unit(n)
     state = []
     lowest = None
     for a in mats:
         back, normal, scale = start(a)
         least = (0.99 * BROADENING**2) * scale
         lowest = least if lowest is None else jnp.minimum(lowest, least)
-        state.append((back, one - normal * scale, least, scale))
+        state.append((back, normal * scale, least, scale))
     lowest = lowest[0, 0]
     count = jnp.int32(0)
     for value in thresholds():
         count = count + (lowest < value).astype(jnp.int32)
-
-    def step(multiply, _, state):
-        fresh = []
-        for x, rest, least, gain in state:
-            c = 2.0 / (1.0 + least)
-            centred = (1.0 - c) * one + c * rest
-            both = multiply(jnp.concatenate([x, centred], 0), centred)
-            fresh.append((x + both[:n], both[n:], jnp.minimum(c * c * least, 1.0), c * gain))
-        return tuple(fresh)
-
-    state = tuple(state)
-    for k in range(FULL_STEPS):
-        state = step(mul_full, k, state)
-    middle = jnp.maximum(count - (FULL_STEPS + LOW_STEPS), 0)
-    state = lax.fori_loop(0, middle, functools.partial(step, mul_split), state)
-    state = lax.fori_loop(0, LOW_STEPS, functools.partial(step, mul_low), state)
+    state = lax.fori_loop(0, jnp.maximum(count - LATE_STEPS, 0), early_step, tuple(state))
+    one = unit(mats[0].shape[0])
+    state = tuple((x, one - d, least, gain) for x, d, least, gain in state)
+    for _ in range(LATE_STEPS):
+        state = late_step(state)
     found, worst = [], jnp.zeros((1, 1), F32)
     for a, (x, _, _, gain) in zip(mats, state):
         x = x * gain
@@ -298,7 +306,7 @@
 
 
 def spread_kernel(links_ref, record_ref, before_ref, out_ref):
-    c0, c1, _, c0h, _, c2h = (links_ref[at] for at in chain_links(False))
+    _, c1, _, c0h, _, c2h = (links_ref[at] for at in chain_links(False))
     b0, b1, b2, t0, p1, p2, q, r = (record_ref[k] for k in range(RECORD))
     w0 = mul(c0h, b0)
     m1 = mul(c1, b2)
@@ -316,14 +324,14 @@
 
 
 def finish_kernel(schur_ref, spread_ref, message_ref, mine_ref, theirs_ref):
-    _, core, right, outer = place()
+    _, _, right, outer = place()
     n = schur_ref.shape[0]
 
     def run(invert):
         closed = schur_ref[...] - mul(mul(spread_ref[9], message_ref[...]), spread_ref[10])
         (full,), bad = invert([closed])
-        reach = mul(jnp.concatenate([spread_ref[3 + j] for j in range(3)], 0), full)
-        green = [spread_ref[j] + mul(reach[j * n : (j + 1) * n], spread_ref[6 + j]) for j in range(3)] + [full]
+        reach = mul_split(jnp.concatenate([spread_ref[3 + j] for j in range(3)], 0), full)
+        green = [spread_ref[j] + mul_split(reach[j * n : (j + 1) * n], spread_ref[6 + j]) for j in range(3)] + [full]
 
         def store(outer_ref, inner_ref):
             for k in range(4):
@@ -350,7 +358,7 @@
 
 
 def combine_kernel(
-    weight_ref, offset_ref, mine_ref, partner_ref, third_a, third_b, pattern_hbm, out_ref, pattern_ref, sem
+    weight_ref, offset_ref, mine_ref, partner_ref, third_ref, pattern_hbm, out_ref, pattern_ref, sem
 ):
     _, core, _, _ = place()
     pltpu.sync_copy(pattern_hbm, pattern_ref)
@@ -376,12 +384,12 @@
     for k in range(out_ref.shape[1]):
         for part in range(2):
             value = mine_weight * mine_ref[k, part] + partner_weight * partner_ref[k, part]
-            value = value + away_weight * jnp.where(core == 0, third_a[k, part], third_b[k, part])
+            value = value + away_weight * third_ref[k, part]
             out_ref[0, k, part] = value * keep
 
 
 def kernel(body, shapes, where, scratch=(), aliases=None, result="v"):
-    spaces = {"s": pltpu.SMEM, "v": pltpu.VMEM, "a": pl.ANY}
+    spaces = {"s": pltpu.SMEM, "v": pltpu.VMEM, "a": pl.ANY, "h": pltpu.HBM}
     many = len(shapes) > 1
     if result == "v":
         outs = [pltpu.VMEM(shape, F32) for shape in shapes]
@@ -400,7 +408,7 @@
 
     def placed(*operands):
         return call(*(
-            pltpu.with_memory_space_constraint(x, pltpu.VMEM) if w == "v" else x for x, w in zip(operands, where)
+            pltpu.with_memory_space_constraint(x, spaces[w]) if w in "vh" else x for x, w in zip(operands, where)
         ))
 
     return placed
@@ -428,7 +436,7 @@
     cpl_far = lax.ppermute(coupling, "space", swap)
 
     own = kernel(
-        own_kernel, [(4,) + row, (LINKS,) + row], "aaa", [vmem(*pair), vmem(*pair), vmem(2, n, n), sems(3)]
+        own_kernel, [(4,) + row, (LINKS,) + row], "hhh", [vmem(*pair), vmem(*pair), vmem(2, n, n), sems(3)]
     )(ham_diag, coupling, contact_left)
     blocks, links, head, last = kernel(
         join_kernel, [(4,) + row, (LINKS,) + row, row, row], "vvvv", aliases={0: 0, 1: 1}
@@ -437,6 +445,7 @@
         kernel(functools.partial(eliminate_kernel, turned), [(RECORD,) + row, row, row], "vvv")
         for turned in (False, True)
     )
+
     def chip_move(value, pairs):
         return lax.ppermute(value, "space", [(2 * a + k, 2 * b + k) for a, b in pairs for k in range(2)])
 
@@ -460,23 +469,18 @@
         message = jnp.where(depth == d, chip_move(fresh[2], outward), message)
 
     mine, theirs = kernel(finish_kernel, [pair, pair], "vvv")(schur, spread, message)
+    ends_from = [(e + 1 - 2 * (1 - e % 2), e) for e in range(energies)]
+    wanted = [(source, e) for source, e in ends_from if 0 <= source < energies]
+    pairs = []
+    for c in range(chips):
+        for source, e in wanted:
+            for k, site in enumerate((source + 1 - 2 * (source % 2), (source + energies // 2) % energies)):
+                pairs.append(((2 * c + k) * energies + site, (2 * c + k) * energies + e))
+    third = lax.ppermute(mine, ("space", "energy"), pairs)
     partner = lax.ppermute(theirs, "space", swap)
-
-    def flat(p, e):
-        return p * energies + e
-
-    hops = [(e - 2, e) for e in range(2, energies, 2)] + [(e + 2, e) for e in range(1, energies - 2, 2)]
-    third = [
-        lax.ppermute(
-            mine if k == 0 else theirs,
-            ("space", "energy"),
-            [(flat(2 * c, a), flat(2 * c + k, b)) for c in range(chips) for a, b in hops],
-        )
-        for k in range(2)
-    ]
     return kernel(
-        combine_kernel, [(1,) + pair], "ssvvvva", [pltpu.VMEM(pattern.shape, jnp.int32), sems(1)], result="a"
-    )(mode_weight, mode_offset, mine, partner, third[0], third[1], pattern)
+        combine_kernel, [(1,) + pair], "ssvvva", [pltpu.VMEM(pattern.shape, jnp.int32), sems(1)], result="a"
+    )(mode_weight, mode_offset, mine, partner, third, pattern)
 
 
 def solution(mesh):

time: 50.2 us -> 45.5 us (0.906)
  local copies, waits for them, and re-layouts: 2.82 us -> 0.02 us
  Pallas kernels: 27.7 us -> 25.4 us
  waiting for transfers between devices: 8.67 us -> 10.4 us
  starting transfers between devices: 10.4 us -> 9.23 us
    unnamed x12 -> x6, local copies, waits for them, and re-layouts: 2.82 us -> 0.02 us
    pallas_call x6, Pallas kernels: 27.7 us -> 25.4 us  [placed(): call(*(pltpu.with_memory_space_constraint(x, spaces[w]) if w in 'vh' else...]
    ppermute x2 -> x1, waiting for transfers between devices: 5.27 us -> 6.5 us  [on_device(): third = lax.ppermute(mine, ('space', 'energy'), pairs)]
    ppermute x2 -> x1, starting transfers between devices: 4.86 us -> 3.78 us  [on_device(): third = lax.ppermute(mine, ('space', 'energy'), pairs)]
  transfers between devices with their start and end apart: 7 -> 6, of which waited for: 3 -> 3; matrix products, arithmetic and copies ran while one was open for 0% -> 0% of each run, Pallas kernels for 38% -> 40%
where the time goes in v1:
time: 45.5 us; the launch traced here: 45.4 us
  Pallas kernels  25.4 us (56%)
  waiting for transfers between devices  10.4 us (23%)
  starting transfers between devices  9.23 us (20%)
    pallas_call x6, Pallas kernels, placed(): call(*(pltpu.with_memory_space_constraint(x, spaces[w]) if w in 'vh' else...  25.4 us
    ppermute x1, waiting for transfers between devices, on_device(): third = lax.ppermute(mine, ('space', 'energy'), pairs)  6.5 us
    ppermute x2, starting transfers between devices, chip_move(): lax.ppermute(value, 'space', [(2 * a + k, 2 * b + k) for a, b in pairs fo...  4.86 us
    ppermute x1, starting transfers between devices, on_device(): third = lax.ppermute(mine, ('space', 'energy'), pairs)  3.78 us
    ppermute x2, waiting for transfers between devices, chip_move(): lax.ppermute(value, 'space', [(2 * a + k, 2 * b + k) for a, b in pairs fo...  3.54 us
  transfers between devices with their start and end apart: 6, of which 3 were waited for; matrix products, arithmetic and copies ran while one was open for 0% of the time, Pallas kernels for 40%

profile of v1, /device:TPU:0, one launch (start us, length us, event | category | flops | bytes accessed | tf_op | source)
XLA Modules:
  0.0 45.4 jit_solution(3101088436487074831)
XLA Ops:
  0.0 0.5 %collective-permute-start = (f32[2,2,128,128]{3,2,1,0:T(8,128)}, f32[2,2,128,128]{3,2,1,0:T(8,128)S(1)}, u32[]{:S(2)}, u32[]{:S(2)}) collective-permute-start(f32[2,2,128,128]{3,2,1,0:T(8,128)} %ham_hbm.1), channel_id=1, source_target_pairs={{0,8},{8,0},{16,24},{24,16},{1,9},{9,1},{17,25},{25,17},{2,10},{10... | collective-permute-start | bytes 786440 | tf_op jit(solution)/shard_map/ppermute | solution.py:435
  0.5 0.0 collective-permute-start.1
  0.5 1.3 %shard_map.64 = (f32[4,128,256]{2,1,0:T(8,128)S(1)}, f32[10,128,256]{2,1,0:T(8,128)S(1)}) custom-call(f32[2,2,128,128]{3,2,1,0:T(8,128)} %ham_hbm.1, f32[2,2,128,128]{3,2,1,0:T(8,128)} %cpl_hbm.1, f32[2,128,128]{2,1,0:T(8,128)} %contact_hbm.1), custom_call_target="tpu_custom_call" | custom-call | tf_op jit(solution)/shard_map/pallas_call | solution.py:410
  1.8 0.0 collective-permute-done.ham
  1.9 0.4 collective-permute-done.1.cpl
  2.2 0.4 shard_map.65
  2.6 4.8 %collective-permute-start.2 = (f32[128,256]{1,0:T(8,128)S(1)}, f32[128,256]{1,0:T(8,128)S(1)}, u32[]{:S(2)}, u32[]{:S(2)}) collective-permute-start(f32[128,256]{1,0:T(8,128)S(1)} %get-tuple-element.23), channel_id=1, source_target_pairs={{0,16},{8,24},{1,17},{9,25},{2,18},{10,26},{3,19},{11,27},{4,20},{... | collective-permute-start | bytes 393224 | tf_op jit(solution)/shard_map/ppermute | solution.py:450
  7.4 15.3 %shard_map.66 = (f32[8,128,256]{2,1,0:T(8,128)S(1)}, f32[128,256]{1,0:T(8,128)S(1)}, f32[128,256]{1,0:T(8,128)S(1)}) custom-call(f32[4,128,256]{2,1,0:T(8,128)S(1)} %get-tuple-element.18.blocks_ref, f32[10,128,256]{2,1,0:T(8,128)S(1)} %get-tuple-element.19.links_ref, f32[128,256]{1,0:T(8,128)S(1)} %get-tuple-element.20.head_ref), custom_call_target="tpu_custom_call" | custom-call | tf_op jit(solution)/shard_map/pallas_call | solution.py:410
  22.7 0.1 collective-permute-start.3
  22.8 0.0 collective-permute-done.2.before_ref
  22.8 1.6 %shard_map.67.spread_ref = f32[11,128,256]{2,1,0:T(8,128)S(1)} custom-call(f32[10,128,256]{2,1,0:T(8,128)S(1)} %get-tuple-element.19.links_ref, f32[8,128,256]{2,1,0:T(8,128)S(1)} %get-tuple-element.22.record_ref, f32[128,256]{1,0:T(8,128)S(1)} %collective-permute-done.2.before_ref), custom_call_target="tpu_custom_call" | custom-call | tf_op jit(solution)/shard_map/pallas_call | solution.py:410
  24.5 0.0 copy-start
  24.5 0.0 copy-start.1
  24.5 0.0 copy-start.2
  24.5 3.5 %collective-permute-done.3.message_ref = f32[128,256]{1,0:T(8,128)S(1)} collective-permute-done((f32[128,256]{1,0:T(8,128)S(1)}, f32[128,256]{1,0:T(8,128)S(1)}, u32[]{:S(2)}, u32[]{:S(2)}) %collective-permute-start.3) | collective-permute-done | bytes 131104 | tf_op jit(solution)/shard_map/ppermute | solution.py:450
  28.1 5.3 %shard_map.68 = (f32[2,2,128,128]{3,2,1,0:T(8,128)S(1)}, f32[2,2,128,128]{3,2,1,0:T(8,128)S(1)}) custom-call(f32[128,256]{1,0:T(8,128)S(1)} %get-tuple-element.21.schur_ref, f32[11,128,256]{2,1,0:T(8,128)S(1)} %shard_map.67.spread_ref, f32[128,256]{1,0:T(8,128)S(1)} %collective-permute-done.3.message_ref), custom_call_target="tpu_custom_call" | custom-call | tf_op jit(solution)/shard_map/pallas_call | solution.py:410
  33.4 0.1 collective-permute-start.4
  33.5 3.8 %collective-permute-start.5 = (f32[2,2,128,128]{3,2,1,0:T(8,128)S(1)}, f32[2,2,128,128]{3,2,1,0:T(8,128)S(1)}, u32[]{:S(2)}, u32[]{:S(2)}) collective-permute-start(f32[2,2,128,128]{3,2,1,0:T(8,128)S(1)} %get-tuple-element.25.mine_ref), channel_id=1, source_target_pairs={{3,1},{14,9},{0,2},{13,10},{5,3},{8,11},{2,4},{15,12},{7,5},{10,13... | collective-permute-start | bytes 786440 | tf_op jit(solution)/shard_map/ppermute | solution.py:479
  37.3 0.0 collective-permute-done.4.partner_ref
  37.3 6.5 %collective-permute-done.5.third_ref = f32[2,2,128,128]{3,2,1,0:T(8,128)S(1)} collective-permute-done((f32[2,2,128,128]{3,2,1,0:T(8,128)S(1)}, f32[2,2,128,128]{3,2,1,0:T(8,128)S(1)}, u32[]{:S(2)}, u32[]{:S(2)}) %collective-permute-start.5) | collective-permute-done | bytes 262176 | tf_op jit(solution)/shard_map/ppermute | solution.py:479
  43.8 0.0 copy-done
  43.8 0.0 copy-done.1
  43.8 0.0 copy-done.2
  43.8 1.4 %shard_map.69 = f32[1,2,2,128,128]{4,3,2,1,0:T(8,128)} custom-call(f32[4]{0:T(128)S(1)} %copy-done.1, s32[4]{0:T(128)S(1)} %copy-done.2, f32[2,2,128,128]{3,2,1,0:T(8,128)S(1)} %get-tuple-element.25.mine_ref, f32[2,2,128,128]{3,2,1,0:T(8,128)S(1)} %collective-permute-done.4.partner_ref, f32[2,2,128,128]{3,2,1,0:T(8,128)S(1)} %collective-permute-done.5.third_ref, ...), custom_call_target="tpu_custom_call" | custom-call | tf_op jit(solution)/shard_map/pallas_call | solution.py:410
Async XLA Ops:
  0.0 1.9 %collective-permute-start = (f32[2,2,128,128]{3,2,1,0:T(8,128)}, f32[2,2,128,128]{3,2,1,0:T(8,128)S(1)}, u32[]{:S(2)}, u32[]{:S(2)}) collective-permute-start(f32[2,2,128,128]{3,2,1,0:T(8,128)} %ham_hbm.1), channel_id=1, source_target_pairs={{0,8},{8,0},{16,24},{24,16},{1,9},{9,1},{17,25},{25,17},{2,10},{10... | collective-permute-start | bytes 786440 | tf_op jit(solution)/shard_map/ppermute | solution.py:435
  0.5 1.7 %collective-permute-start.1 = (f32[2,2,128,128]{3,2,1,0:T(8,128)}, f32[2,2,128,128]{3,2,1,0:T(8,128)S(1)}, u32[]{:S(2)}, u32[]{:S(2)}) collective-permute-start(f32[2,2,128,128]{3,2,1,0:T(8,128)} %cpl_hbm.1), channel_id=1, source_target_pairs={{0,8},{8,0},{16,24},{24,16},{1,9},{9,1},{17,25},{25,17},{2,10},{10... | collective-permute-start | bytes 786440 | tf_op jit(solution)/shard_map/ppermute | solution.py:436
  2.6 20.2 %collective-permute-start.2 = (f32[128,256]{1,0:T(8,128)S(1)}, f32[128,256]{1,0:T(8,128)S(1)}, u32[]{:S(2)}, u32[]{:S(2)}) collective-permute-start(f32[128,256]{1,0:T(8,128)S(1)} %get-tuple-element.23), channel_id=1, source_target_pairs={{0,16},{8,24},{1,17},{9,25},{2,18},{10,26},{3,19},{11,27},{4,20},{... | collective-permute-start | bytes 393224 | tf_op jit(solution)/shard_map/ppermute | solution.py:450
  22.7 5.3 %collective-permute-start.3 = (f32[128,256]{1,0:T(8,128)S(1)}, f32[128,256]{1,0:T(8,128)S(1)}, u32[]{:S(2)}, u32[]{:S(2)}) collective-permute-start(f32[128,256]{1,0:T(8,128)S(1)} %get-tuple-element.24), channel_id=1, source_target_pairs={{0,16},{8,24},{16,0},{24,8},{1,17},{9,25},{17,1},{25,9},{2,18},{10... | collective-permute-start | bytes 393224 | tf_op jit(solution)/shard_map/ppermute | solution.py:450
  24.5 19.3 %copy-start = (s32[128,128]{1,0:T(8,128)S(1)}, s32[128,128]{1,0:T(8,128)}, u32[]{:S(2)}) copy-start(s32[128,128]{1,0:T(8,128)} %pattern_hbm.1) | copy-start | bytes 196612
  24.5 19.3 %copy-start.1 = (f32[4]{0:T(128)S(1)}, f32[4]{0:T(128)}, u32[]{:S(2)}) copy-start(f32[4]{0:T(128)} %weight_ref.1) | copy-start | bytes 52
  24.5 19.3 %copy-start.2 = (s32[4]{0:T(128)S(1)}, s32[4]{0:T(128)}, u32[]{:S(2)}) copy-start(s32[4]{0:T(128)} %offset_ref.1) | copy-start | bytes 52
  33.4 3.9 %collective-permute-start.4 = (f32[2,2,128,128]{3,2,1,0:T(8,128)S(1)}, f32[2,2,128,128]{3,2,1,0:T(8,128)S(1)}, u32[]{:S(2)}, u32[]{:S(2)}) collective-permute-start(f32[2,2,128,128]{3,2,1,0:T(8,128)S(1)} %get-tuple-element.26), channel_id=1, source_target_pairs={{0,8},{8,0},{16,24},{24,16},{1,9},{9,1},{17,25},{25,17},{2,10},{10... | collective-permute-start | bytes 786440 | tf_op jit(solution)/shard_map/ppermute | solution.py:480
  33.5 10.3 %collective-permute-start.5 = (f32[2,2,128,128]{3,2,1,0:T(8,128)S(1)}, f32[2,2,128,128]{3,2,1,0:T(8,128)S(1)}, u32[]{:S(2)}, u32[]{:S(2)}) collective-permute-start(f32[2,2,128,128]{3,2,1,0:T(8,128)S(1)} %get-tuple-element.25.mine_ref), channel_id=1, source_target_pairs={{3,1},{14,9},{0,2},{13,10},{5,3},{8,11},{2,4},{15,12},{7,5},{10,13... | collective-permute-start | bytes 786440 | tf_op jit(solution)/shard_map/ppermute | solution.py:479

commit v2 on v1

--- a/solution.py
+++ b/solution.py
@@ -15,6 +15,7 @@
 BF16 = jnp.bfloat16
 
 
+FIXED_STEPS = (8, 7)
 LATE_STEPS = 2
 MOST_STEPS = 20
 SETTLED = 0.999
@@ -42,10 +43,12 @@
 
 
 def mul_split(a, b):
+    m = a.shape[0]
     a_high, a_low = halves(a)
     b_high, b_low = halves(b)
     b_high, b_low = operand(b_high), operand(b_low)
-    return dot(a_high, b_high) + (dot(a_high, b_low) + dot(a_low, b_high))
+    both = dot(jnp.concatenate([a_high, a_low], 0), b_high)
+    return both[:m] + (both[m:] + dot(a_high, b_low))
 
 
 def mul_low(a, b):
@@ -76,10 +79,13 @@
 
 
 def start(a):
+    n = a.shape[0]
     back = adj(a)
-    normal = mul_full(a, back)
-    scale = 1.0 / jnp.sqrt(total(normal * normal))
-    return back, normal, scale
+    normal = mul_split(a, back)
+    size = jnp.sqrt(a[:, :n] * a[:, :n] + a[:, n:] * a[:, n:])
+    across = jnp.max(jnp.sum(size, axis=1, keepdims=True), axis=0, keepdims=True)
+    down = jnp.max(jnp.sum(size, axis=0, keepdims=True), axis=1, keepdims=True)
+    return back, normal, 1.0 / (across * down)
 
 
 def thresholds():
@@ -92,10 +98,10 @@
 def early_step(_, state):
     fresh = []
     for x, d, least, gain in state:
-        n = d.shape[0]
         c = 2.0 / (1.0 + least)
-        both = mul_split(jnp.concatenate([d, x], 0), d)
-        fresh.append((2.0 * x - c * both[n:], c * (2.0 * d - c * both[:n]), jnp.minimum(c * c * least, 1.0), c * gain))
+        square = mul_split(d, d)
+        x = 2.0 * x - c * mul_split(x, d)
+        fresh.append((x, c * (2.0 * d - c * square), jnp.minimum(c * c * least, 1.0), c * gain))
     return tuple(fresh)
 
 
@@ -122,7 +128,10 @@
     count = jnp.int32(0)
     for value in thresholds():
         count = count + (lowest < value).astype(jnp.int32)
-    state = lax.fori_loop(0, jnp.maximum(count - LATE_STEPS, 0), early_step, tuple(state))
+    fixed = FIXED_STEPS[len(mats) - 1]
+    for k in range(fixed):
+        state = early_step(k, state)
+    state = lax.fori_loop(0, jnp.maximum(count - LATE_STEPS - fixed, 0), early_step, tuple(state))
     one = unit(mats[0].shape[0])
     state = tuple((x, one - d, least, gain) for x, d, least, gain in state)
     for _ in range(LATE_STEPS):
@@ -223,13 +232,12 @@
     links_ref[CONTACT + 1] = adj(lead)
 
 
-def join_kernel(own_blocks, own_links, ham, cpl, blocks_ref, links_ref, head_ref, last_ref):
+def join_kernel(own_blocks, own_links, ham, cpl, blocks_ref, links_ref, head_ref):
     _, core, right, _ = place()
     fill(ham, cpl, 2, blocks_ref, links_ref)
     end = chip_index(3, core)
     lead = links_ref[jnp.where(right == 1, BACK + end, CONTACT)]
     lead_back = links_ref[jnp.where(right == 1, end, CONTACT + 1)]
-    last_ref[...] = links_ref[end]
     head_ref[...] = times_half_imag(mul(lead, lead_back))
 
 
@@ -266,29 +274,36 @@
     return jnp.maximum(bad, more)
 
 
-def chip_ends(links_ref, before_ref):
+def send(links_ref, corner_ref, sender):
     _, core, right, _ = place()
-    ahead = before_ref[...]
-    back = adj(ahead)
     end = chip_index(3, core)
-    last, last_back = links_ref[end], links_ref[BACK + end]
-    mirrored = right == 1
-    pick = lambda a, b: jnp.where(mirrored, a, b)
-    return [pick(last, back), pick(last_back, ahead), pick(back, last), pick(ahead, last_back)]
-
-
-def ends_kernel(links_ref, before_ref, out_ref):
-    for k, value in enumerate(chip_ends(links_ref, before_ref)):
-        out_ref[k] = value
-
-
-def head_kernel(link_ref, back_ref, message_ref, out_ref):
-    out_ref[...] = -mul(mul(link_ref[...], message_ref[...]), back_ref[...])
+
+    @pl.when(right == sender)
+    def _():
+        corner_ref[...] = mul(mul(links_ref[BACK + end], corner_ref[...]), links_ref[end])
+
+
+def receive(links_ref, message_ref, sigma_ref, multiplies):
+    _, core, right, _ = place()
+    end = chip_index(3, core)
+
+    @pl.when(right == multiplies)
+    def _():
+        sigma_ref[...] = mul(mul(links_ref[end], message_ref[...]), links_ref[BACK + end])
+
+    @pl.when(right != multiplies)
+    def _():
+        sigma_ref[...] = message_ref[...]
+
+
+def head_kernel(multiplies, links_ref, message_ref, out_ref):
+    receive(links_ref, message_ref, out_ref, multiplies)
+    out_ref[...] = -out_ref[...]
 
 
 def eliminate_kernel(turned, blocks_ref, links_ref, head_ref, record_ref, schur_ref, corner_ref):
     def run(invert):
-        return eliminate(
+        bad = eliminate(
             [blocks_ref[block_index(3 - k if turned else k)] for k in range(4)],
             [links_ref[at] for at in chain_links(turned)],
             head_ref[...],
@@ -297,6 +312,8 @@
             corner_ref,
             invert,
         )
+        send(links_ref, corner_ref, 1 if turned else 0)
+        return bad
 
     bad = jnp.sum(run(invert_fast))
 
@@ -305,7 +322,7 @@
         run(invert_safe)
 
 
-def spread_kernel(links_ref, record_ref, before_ref, out_ref):
+def spread_kernel(links_ref, record_ref, out_ref):
     _, c1, _, c0h, _, c2h = (links_ref[at] for at in chain_links(False))
     b0, b1, b2, t0, p1, p2, q, r = (record_ref[k] for k in range(RECORD))
     w0 = mul(c0h, b0)
@@ -320,15 +337,15 @@
     out_ref[6] = mul(r, w0)
     out_ref[7] = r
     out_ref[8] = mul(r, m1) + m2
-    _, _, out_ref[9], out_ref[10] = chip_ends(links_ref, before_ref)
-
-
-def finish_kernel(schur_ref, spread_ref, message_ref, mine_ref, theirs_ref):
+
+
+def finish_kernel(schur_ref, spread_ref, links_ref, message_ref, mine_ref, theirs_ref, sigma_ref):
     _, _, right, outer = place()
     n = schur_ref.shape[0]
+    receive(links_ref, message_ref, sigma_ref, 0)
 
     def run(invert):
-        closed = schur_ref[...] - mul(mul(spread_ref[9], message_ref[...]), spread_ref[10])
+        closed = schur_ref[...] - sigma_ref[...]
         (full,), bad = invert([closed])
         reach = mul_split(jnp.concatenate([spread_ref[3 + j] for j in range(3)], 0), full)
         green = [spread_ref[j] + mul_split(reach[j * n : (j + 1) * n], spread_ref[6 + j]) for j in range(3)] + [full]
@@ -358,10 +375,9 @@
 
 
 def combine_kernel(
-    weight_ref, offset_ref, mine_ref, partner_ref, third_ref, pattern_hbm, out_ref, pattern_ref, sem
+    weight_ref, offset_ref, mine_ref, partner_ref, third_ref, pattern_ref, out_ref
 ):
     _, core, _, _ = place()
-    pltpu.sync_copy(pattern_hbm, pattern_ref)
     energy_count = lax.axis_size("energy")
     rank = lax.axis_index("energy")
     half = energy_count // 2
@@ -438,8 +454,8 @@
     own = kernel(
         own_kernel, [(4,) + row, (LINKS,) + row], "hhh", [vmem(*pair), vmem(*pair), vmem(2, n, n), sems(3)]
     )(ham_diag, coupling, contact_left)
-    blocks, links, head, last = kernel(
-        join_kernel, [(4,) + row, (LINKS,) + row, row, row], "vvvv", aliases={0: 0, 1: 1}
+    blocks, links, head = kernel(
+        join_kernel, [(4,) + row, (LINKS,) + row, row], "vvvv", aliases={0: 0, 1: 1}
     )(*own, ham_far, cpl_far)
     forward, backward = (
         kernel(functools.partial(eliminate_kernel, turned), [(RECORD,) + row, row, row], "vvv")
@@ -449,26 +465,27 @@
     def chip_move(value, pairs):
         return lax.ppermute(value, "space", [(2 * a + k, 2 * b + k) for a, b in pairs for k in range(2)])
 
-    before = chip_move(last, [(c, c + 1) for c in range(chips - 1)])
     state = forward(blocks, links, head)
 
-    if middle > 1:
-        ends = kernel(ends_kernel, [(4,) + row], "vv")(links, before)
-        head_of = kernel(head_kernel, [row], "vvv")
+    head_inward, head_outward = (
+        kernel(functools.partial(head_kernel, multiplies), [row], "vv") for multiplies in (1, 0)
+    )
     for d in range(1, middle):
         inward = [(c, c + 1) for c in range(middle - 1)] + [(c + 1, c) for c in range(middle, chips - 1)]
-        fresh = forward(blocks, links, head_of(ends[0], ends[1], chip_move(state[2], inward)))
+        fresh = forward(blocks, links, head_inward(links, chip_move(state[2], inward)))
         state = [jnp.where(depth >= d, a, b) for a, b in zip(fresh, state)]
     record, schur, corner = state
 
     message = chip_move(corner, [(middle - 1, middle), (middle, middle - 1)])
-    spread = kernel(spread_kernel, [(11,) + row], "vvv")(links, record, before)
+    spread = kernel(spread_kernel, [(9,) + row], "vv")(links, record)
     for d in range(middle - 2, -1, -1):
         outward = [(c + 1, c) for c in range(middle - 1)] + [(c, c + 1) for c in range(middle, chips - 1)]
-        fresh = backward(blocks, links, head_of(ends[2], ends[3], message))
+        fresh = backward(blocks, links, head_outward(links, message))
         message = jnp.where(depth == d, chip_move(fresh[2], outward), message)
 
-    mine, theirs = kernel(finish_kernel, [pair, pair], "vvv")(schur, spread, message)
+    mine, theirs = kernel(finish_kernel, [pair, pair], "vvvv", [vmem(*row)])(
+        schur, spread, links, message
+    )
     ends_from = [(e + 1 - 2 * (1 - e % 2), e) for e in range(energies)]
     wanted = [(source, e) for source, e in ends_from if 0 <= source < energies]
     pairs = []
@@ -479,7 +496,7 @@
     third = lax.ppermute(mine, ("space", "energy"), pairs)
     partner = lax.ppermute(theirs, "space", swap)
     return kernel(
-        combine_kernel, [(1,) + pair], "ssvvva", [pltpu.VMEM(pattern.shape, jnp.int32), sems(1)], result="a"
+        combine_kernel, [(1,) + pair], "ssvvvv", result="a"
     )(mode_weight, mode_offset, mine, partner, third, pattern)
 
 

time: 45.5 us -> 222 us (4.88)
  the two profiles are of different devices: /device:TPU:0 before, /device:TPU:3 now
where the time goes in v2:
time: 222 us; the launch traced here: 221 us
  Pallas kernels  208 us (94%)
  waiting for transfers between devices  10.4 us (5%)
  starting transfers between devices  2.74 us (1%)
    pallas_call x6, Pallas kernels, placed(): call(*(pltpu.with_memory_space_constraint(x, spaces[w]) if w in 'vh' else...  208 us
    ppermute x1, waiting for transfers between devices, on_device(): third = lax.ppermute(mine, ('space', 'energy'), pairs)  7.87 us
  transfers between devices with their start and end apart: 5, of which 3 were waited for; matrix products, arithmetic and copies ran while one was open for 0% of the time, Pallas kernels for 1%

profile of v2, /device:TPU:3, one launch (start us, length us, event | category | flops | bytes accessed | tf_op | source)
XLA Modules:
  0.0 221.4 jit_solution(534965622591126308)
XLA Ops:
  0.0 0.7 collective-permute-start
  0.7 0.0 collective-permute-start.1
  0.7 1.3 shard_map.64
  2.0 0.0 collective-permute-done.ham
  2.0 0.4 collective-permute-done.1.cpl
  2.4 0.4 shard_map.65
  2.8 197.9 %shard_map.66 = (f32[8,128,256]{2,1,0:T(8,128)S(1)}, f32[128,256]{1,0:T(8,128)S(1)}, f32[128,256]{1,0:T(8,128)S(1)}) custom-call(f32[4,128,256]{2,1,0:T(8,128)S(1)} %get-tuple-element.17.blocks_ref, f32[10,128,256]{2,1,0:T(8,128)S(1)} %get-tuple-element.18.links_ref, f32[128,256]{1,0:T(8,128)S(1)} %get-tuple-element.19.head_ref), custom_call_target="tpu_custom_call" | custom-call | tf_op jit(solution)/shard_map/pallas_call | solution.py:426
  200.7 0.1 collective-permute-start.2
  200.8 1.6 shard_map.67.spread_ref
  202.4 2.2 collective-permute-done.2.message_ref
  204.6 0.0 copy-start
  204.6 0.0 copy-start.1
  204.6 0.0 copy-start.2
  204.6 5.5 %shard_map.68 = (f32[2,2,128,128]{3,2,1,0:T(8,128)S(1)}, f32[2,2,128,128]{3,2,1,0:T(8,128)S(1)}) custom-call(f32[128,256]{1,0:T(8,128)S(1)} %get-tuple-element.20.schur_ref, f32[9,128,256]{2,1,0:T(8,128)S(1)} %shard_map.67.spread_ref, f32[10,128,256]{2,1,0:T(8,128)S(1)} %get-tuple-element.18.links_ref, f32[128,256]{1,0:T(8,128)S(1)} %collective-permute-done.2.message_ref), custom_call_target="tpu_custom_call" | custom-call | tf_op jit(solution)/shard_map/pallas_call | solution.py:426
  210.1 0.1 collective-permute-start.3
  210.2 1.9 collective-permute-start.4
  212.1 0.0 collective-permute-done.3.partner_ref
  212.2 7.9 %collective-permute-done.4.third_ref = f32[2,2,128,128]{3,2,1,0:T(8,128)S(1)} collective-permute-done((f32[2,2,128,128]{3,2,1,0:T(8,128)S(1)}, f32[2,2,128,128]{3,2,1,0:T(8,128)S(1)}, u32[]{:S(2)}, u32[]{:S(2)}) %collective-permute-start.4) | collective-permute-done | bytes 262176 | tf_op jit(solution)/shard_map/ppermute | solution.py:496
  220.0 0.0 copy-done
  220.0 0.0 copy-done.1
  220.0 0.0 copy-done.2
  220.0 1.3 shard_map.69
Async XLA Ops:
  0.0 2.0 collective-permute-start
  0.7 1.7 collective-permute-start.1
  200.7 3.9 %collective-permute-start.2 = (f32[128,256]{1,0:T(8,128)S(1)}, f32[128,256]{1,0:T(8,128)S(1)}, u32[]{:S(2)}, u32[]{:S(2)}) collective-permute-start(f32[128,256]{1,0:T(8,128)S(1)} %get-tuple-element.22), channel_id=1, source_target_pairs={{0,16},{8,24},{16,0},{24,8},{1,17},{9,25},{17,1},{25,9},{2,18},{10... | collective-permute-start | bytes 393224 | tf_op jit(solution)/shard_map/ppermute | solution.py:466
  204.6 15.4 %copy-start = (s32[128,128]{1,0:T(8,128)S(1)}, s32[128,128]{1,0:T(8,128)}, u32[]{:S(2)}) copy-start(s32[128,128]{1,0:T(8,128)} %pattern_ref.1) | copy-start | bytes 196612
  204.6 15.5 %copy-start.1 = (f32[4]{0:T(128)S(1)}, f32[4]{0:T(128)}, u32[]{:S(2)}) copy-start(f32[4]{0:T(128)} %weight_ref.1) | copy-start | bytes 52
  204.6 15.5 %copy-start.2 = (s32[4]{0:T(128)S(1)}, s32[4]{0:T(128)}, u32[]{:S(2)}) copy-start(s32[4]{0:T(128)} %offset_ref.1) | copy-start | bytes 52
  210.1 2.0 collective-permute-start.3
  210.2 9.8 %collective-permute-start.4 = (f32[2,2,128,128]{3,2,1,0:T(8,128)S(1)}, f32[2,2,128,128]{3,2,1,0:T(8,128)S(1)}, u32[]{:S(2)}, u32[]{:S(2)}) collective-permute-start(f32[2,2,128,128]{3,2,1,0:T(8,128)S(1)} %get-tuple-element.23.mine_ref), channel_id=1, source_target_pairs={{3,1},{14,9},{0,2},{13,10},{5,3},{8,11},{2,4},{15,12},{7,5},{10,13... | collective-permute-start | bytes 786440 | tf_op jit(solution)/shard_map/ppermute | solution.py:496

commit v3 on v2

--- a/solution.py
+++ b/solution.py
@@ -15,7 +15,7 @@
 BF16 = jnp.bfloat16
 
 
-FIXED_STEPS = (8, 7)
+FIXED_STEPS = (7, 5)
 LATE_STEPS = 2
 MOST_STEPS = 20
 SETTLED = 0.999
@@ -102,6 +102,18 @@
         square = mul_split(d, d)
         x = 2.0 * x - c * mul_split(x, d)
         fresh.append((x, c * (2.0 * d - c * square), jnp.minimum(c * c * least, 1.0), c * gain))
+    return tuple(fresh)
+
+
+def first_step(state):
+    fresh = []
+    for x, d, least, gain in state:
+        square = mul_split(d, d)
+        most = 1.0001 * jnp.sqrt(jnp.sqrt(total(square * square)))
+        c = 2.0 / (most + least)
+        x = 2.0 * x - c * mul_split(x, d)
+        low = c * least
+        fresh.append((x, c * (2.0 * d - c * square), jnp.minimum(low * (2.0 - low), 1.0), c * gain))
     return tuple(fresh)
 
 
@@ -118,13 +130,11 @@
 
 def invert_fast(mats):
     state = []
-    lowest = None
     for a in mats:
         back, normal, scale = start(a)
-        least = (0.99 * BROADENING**2) * scale
-        lowest = least if lowest is None else jnp.minimum(lowest, least)
-        state.append((back, normal * scale, least, scale))
-    lowest = lowest[0, 0]
+        state.append((back, normal * scale, (0.99 * BROADENING**2) * scale, scale))
+    state = first_step(state)
+    lowest = functools.reduce(jnp.minimum, [least for _, _, least, _ in state])[0, 0]
     count = jnp.int32(0)
     for value in thresholds():
         count = count + (lowest < value).astype(jnp.int32)
@@ -258,10 +268,12 @@
     p1 = mul(b2, c1h)
     p2 = mul(b2, c2)
     record[B0], record[B2], record[T0], record[P1], record[P2] = b0, b2, t0, p1, p2
-    middle = blocks[1] - mul(c0h, t0) - mul(c1, p1)
-    upper = mul(c1, p2)
-    lower = mul(c2h, p1)
-    tail = blocks[3] - mul(c2h, p2)
+    behind = mul(jnp.concatenate([c1, c2h], 0), p1)
+    middle = blocks[1] - mul(c0h, t0) - behind[: c1.shape[0]]
+    lower = behind[c1.shape[0] :]
+    ahead = mul(jnp.concatenate([c1, c2h], 0), p2)
+    upper = ahead[: c1.shape[0]]
+    tail = blocks[3] - ahead[c1.shape[0] :]
     (b1,), more = invert([middle])
     bad = jnp.maximum(bad, more)
     q = mul(b1, upper)

time: 222 us -> 41 us (0.18)
  the two profiles are of different devices: /device:TPU:3 before, /device:TPU:0 now
where the time goes in v3:
time: 41 us; the launch traced here: 40.8 us
  Pallas kernels  24.4 us (60%)
  waiting for transfers between devices  9.35 us (23%)
  starting transfers between devices  6.95 us (17%)
    pallas_call x6, Pallas kernels, placed(): call(*(pltpu.with_memory_space_constraint(x, spaces[w]) if w in 'vh' else...  24.4 us
    ppermute x1, waiting for transfers between devices, on_device(): third = lax.ppermute(mine, ('space', 'energy'), pairs)  6.51 us
    ppermute x1, starting transfers between devices, on_device(): third = lax.ppermute(mine, ('space', 'energy'), pairs)  4.54 us
    ppermute x1, waiting for transfers between devices, chip_move(): lax.ppermute(value, 'space', [(2 * a + k, 2 * b + k) for a, b in pairs fo...  2.44 us
    ppermute x1, starting transfers between devices, chip_move(): lax.ppermute(value, 'space', [(2 * a + k, 2 * b + k) for a, b in pairs fo...  1.83 us
  transfers between devices with their start and end apart: 5, of which 3 were waited for; matrix products, arithmetic and copies ran while one was open for 0% of the time, Pallas kernels for 7%

profile of v3, /device:TPU:0, one launch (start us, length us, event | category | flops | bytes accessed | tf_op | source)
XLA Modules:
  0.0 40.8 jit_solution(8806495599275733057)
XLA Ops:
  0.0 0.5 %collective-permute-start = (f32[2,2,128,128]{3,2,1,0:T(8,128)}, f32[2,2,128,128]{3,2,1,0:T(8,128)S(1)}, u32[]{:S(2)}, u32[]{:S(2)}) collective-permute-start(f32[2,2,128,128]{3,2,1,0:T(8,128)} %ham_hbm.1), channel_id=1, source_target_pairs={{0,8},{8,0},{16,24},{24,16},{1,9},{9,1},{17,25},{25,17},{2,10},{10... | collective-permute-start | bytes 786440 | tf_op jit(solution)/shard_map/ppermute | solution.py:463
  0.5 0.0 collective-permute-start.1
  0.5 1.3 %shard_map.64 = (f32[4,128,256]{2,1,0:T(8,128)S(1)}, f32[10,128,256]{2,1,0:T(8,128)S(1)}) custom-call(f32[2,2,128,128]{3,2,1,0:T(8,128)} %ham_hbm.1, f32[2,2,128,128]{3,2,1,0:T(8,128)} %cpl_hbm.1, f32[2,128,128]{2,1,0:T(8,128)} %contact_hbm.1), custom_call_target="tpu_custom_call" | custom-call | tf_op jit(solution)/shard_map/pallas_call | solution.py:438
  1.8 0.0 collective-permute-done.ham
  1.9 0.4 collective-permute-done.1.cpl
  2.2 0.4 shard_map.65
  2.6 14.6 %shard_map.66 = (f32[8,128,256]{2,1,0:T(8,128)S(1)}, f32[128,256]{1,0:T(8,128)S(1)}, f32[128,256]{1,0:T(8,128)S(1)}) custom-call(f32[4,128,256]{2,1,0:T(8,128)S(1)} %get-tuple-element.17.blocks_ref, f32[10,128,256]{2,1,0:T(8,128)S(1)} %get-tuple-element.18.links_ref, f32[128,256]{1,0:T(8,128)S(1)} %get-tuple-element.19.head_ref), custom_call_target="tpu_custom_call" | custom-call | tf_op jit(solution)/shard_map/pallas_call | solution.py:438
  17.3 1.8 %collective-permute-start.2 = (f32[128,256]{1,0:T(8,128)S(1)}, f32[128,256]{1,0:T(8,128)S(1)}, u32[]{:S(2)}, u32[]{:S(2)}) collective-permute-start(f32[128,256]{1,0:T(8,128)S(1)} %get-tuple-element.22), channel_id=1, source_target_pairs={{0,16},{8,24},{16,0},{24,8},{1,17},{9,25},{17,1},{25,9},{2,18},{10... | collective-permute-start | bytes 393224 | tf_op jit(solution)/shard_map/ppermute | solution.py:478
  19.1 1.6 %shard_map.67.spread_ref = f32[9,128,256]{2,1,0:T(8,128)S(1)} custom-call(f32[10,128,256]{2,1,0:T(8,128)S(1)} %get-tuple-element.18.links_ref, f32[8,128,256]{2,1,0:T(8,128)S(1)} %get-tuple-element.21.record_ref), custom_call_target="tpu_custom_call" | custom-call | tf_op jit(solution)/shard_map/pallas_call | solution.py:438
  20.8 2.4 %collective-permute-done.2.message_ref = f32[128,256]{1,0:T(8,128)S(1)} collective-permute-done((f32[128,256]{1,0:T(8,128)S(1)}, f32[128,256]{1,0:T(8,128)S(1)}, u32[]{:S(2)}, u32[]{:S(2)}) %collective-permute-start.2) | collective-permute-done | bytes 131104 | tf_op jit(solution)/shard_map/ppermute | solution.py:478
  23.2 0.0 copy-start
  23.2 0.0 copy-start.1
  23.2 0.0 copy-start.2
  23.2 5.1 %shard_map.68 = (f32[2,2,128,128]{3,2,1,0:T(8,128)S(1)}, f32[2,2,128,128]{3,2,1,0:T(8,128)S(1)}) custom-call(f32[128,256]{1,0:T(8,128)S(1)} %get-tuple-element.20.schur_ref, f32[9,128,256]{2,1,0:T(8,128)S(1)} %shard_map.67.spread_ref, f32[10,128,256]{2,1,0:T(8,128)S(1)} %get-tuple-element.18.links_ref, f32[128,256]{1,0:T(8,128)S(1)} %collective-permute-done.2.message_ref), custom_call_target="tpu_custom_call" | custom-call | tf_op jit(solution)/shard_map/pallas_call | solution.py:438
  28.3 0.1 collective-permute-start.3
  28.4 4.5 %collective-permute-start.4 = (f32[2,2,128,128]{3,2,1,0:T(8,128)S(1)}, f32[2,2,128,128]{3,2,1,0:T(8,128)S(1)}, u32[]{:S(2)}, u32[]{:S(2)}) collective-permute-start(f32[2,2,128,128]{3,2,1,0:T(8,128)S(1)} %get-tuple-element.23.mine_ref), channel_id=1, source_target_pairs={{3,1},{14,9},{0,2},{13,10},{5,3},{8,11},{2,4},{15,12},{7,5},{10,13... | collective-permute-start | bytes 786440 | tf_op jit(solution)/shard_map/ppermute | solution.py:508
  32.9 0.0 collective-permute-done.3.partner_ref
  32.9 6.5 %collective-permute-done.4.third_ref = f32[2,2,128,128]{3,2,1,0:T(8,128)S(1)} collective-permute-done((f32[2,2,128,128]{3,2,1,0:T(8,128)S(1)}, f32[2,2,128,128]{3,2,1,0:T(8,128)S(1)}, u32[]{:S(2)}, u32[]{:S(2)}) %collective-permute-start.4) | collective-permute-done | bytes 262176 | tf_op jit(solution)/shard_map/ppermute | solution.py:508
  39.5 0.0 copy-done
  39.5 0.0 copy-done.1
  39.5 0.0 copy-done.2
  39.5 1.3 %shard_map.69 = f32[1,2,2,128,128]{4,3,2,1,0:T(8,128)} custom-call(f32[4]{0:T(128)S(1)} %copy-done.1, s32[4]{0:T(128)S(1)} %copy-done.2, f32[2,2,128,128]{3,2,1,0:T(8,128)S(1)} %get-tuple-element.23.mine_ref, f32[2,2,128,128]{3,2,1,0:T(8,128)S(1)} %collective-permute-done.3.partner_ref, f32[2,2,128,128]{3,2,1,0:T(8,128)S(1)} %collective-permute-done.4.third_ref, ...), custom_call_target="tpu_custom_call" | custom-call | tf_op jit(solution)/shard_map/pallas_call | solution.py:438
Async XLA Ops:
  0.0 1.9 %collective-permute-start = (f32[2,2,128,128]{3,2,1,0:T(8,128)}, f32[2,2,128,128]{3,2,1,0:T(8,128)S(1)}, u32[]{:S(2)}, u32[]{:S(2)}) collective-permute-start(f32[2,2,128,128]{3,2,1,0:T(8,128)} %ham_hbm.1), channel_id=1, source_target_pairs={{0,8},{8,0},{16,24},{24,16},{1,9},{9,1},{17,25},{25,17},{2,10},{10... | collective-permute-start | bytes 786440 | tf_op jit(solution)/shard_map/ppermute | solution.py:463
  0.5 1.7 %collective-permute-start.1 = (f32[2,2,128,128]{3,2,1,0:T(8,128)}, f32[2,2,128,128]{3,2,1,0:T(8,128)S(1)}, u32[]{:S(2)}, u32[]{:S(2)}) collective-permute-start(f32[2,2,128,128]{3,2,1,0:T(8,128)} %cpl_hbm.1), channel_id=1, source_target_pairs={{0,8},{8,0},{16,24},{24,16},{1,9},{9,1},{17,25},{25,17},{2,10},{10... | collective-permute-start | bytes 786440 | tf_op jit(solution)/shard_map/ppermute | solution.py:464
  17.3 5.9 %collective-permute-start.2 = (f32[128,256]{1,0:T(8,128)S(1)}, f32[128,256]{1,0:T(8,128)S(1)}, u32[]{:S(2)}, u32[]{:S(2)}) collective-permute-start(f32[128,256]{1,0:T(8,128)S(1)} %get-tuple-element.22), channel_id=1, source_target_pairs={{0,16},{8,24},{16,0},{24,8},{1,17},{9,25},{17,1},{25,9},{2,18},{10... | collective-permute-start | bytes 393224 | tf_op jit(solution)/shard_map/ppermute | solution.py:478
  23.2 16.2 %copy-start = (s32[128,128]{1,0:T(8,128)S(1)}, s32[128,128]{1,0:T(8,128)}, u32[]{:S(2)}) copy-start(s32[128,128]{1,0:T(8,128)} %pattern_ref.1) | copy-start | bytes 196612
  23.2 16.2 %copy-start.1 = (f32[4]{0:T(128)S(1)}, f32[4]{0:T(128)}, u32[]{:S(2)}) copy-start(f32[4]{0:T(128)} %weight_ref.1) | copy-start | bytes 52
  23.2 16.2 %copy-start.2 = (s32[4]{0:T(128)S(1)}, s32[4]{0:T(128)}, u32[]{:S(2)}) copy-start(s32[4]{0:T(128)} %offset_ref.1) | copy-start | bytes 52
  28.3 4.6 %collective-permute-start.3 = (f32[2,2,128,128]{3,2,1,0:T(8,128)S(1)}, f32[2,2,128,128]{3,2,1,0:T(8,128)S(1)}, u32[]{:S(2)}, u32[]{:S(2)}) collective-permute-start(f32[2,2,128,128]{3,2,1,0:T(8,128)S(1)} %get-tuple-element.24), channel_id=1, source_target_pairs={{0,8},{8,0},{16,24},{24,16},{1,9},{9,1},{17,25},{25,17},{2,10},{10... | collective-permute-start | bytes 786440 | tf_op jit(solution)/shard_map/ppermute | solution.py:509
  28.4 11.1 %collective-permute-start.4 = (f32[2,2,128,128]{3,2,1,0:T(8,128)S(1)}, f32[2,2,128,128]{3,2,1,0:T(8,128)S(1)}, u32[]{:S(2)}, u32[]{:S(2)}) collective-permute-start(f32[2,2,128,128]{3,2,1,0:T(8,128)S(1)} %get-tuple-element.23.mine_ref), channel_id=1, source_target_pairs={{3,1},{14,9},{0,2},{13,10},{5,3},{8,11},{2,4},{15,12},{7,5},{10,13... | collective-permute-start | bytes 786440 | tf_op jit(solution)/shard_map/ppermute | solution.py:508

commit v4 on v3

--- a/solution.py
+++ b/solution.py
@@ -18,7 +18,7 @@
 FIXED_STEPS = (7, 5)
 LATE_STEPS = 2
 MOST_STEPS = 20
-SETTLED = 0.999
+SETTLED = 0.996
 RESIDUE_LIMIT = 4e-3
 SAFE_STEPS = 64
 KERNEL_VMEM = 24 << 20
@@ -334,7 +334,9 @@
         run(invert_safe)
 
 
-def spread_kernel(links_ref, record_ref, out_ref):
+def spread_kernel(weight_ref, offset_ref, links_ref, record_ref, out_ref, weights_ref):
+    for k, value in enumerate(weights(weight_ref, offset_ref)):
+        weights_ref[k] = jnp.full(weights_ref.shape[1:], value, F32)
     _, c1, _, c0h, _, c2h = (links_ref[at] for at in chain_links(False))
     b0, b1, b2, t0, p1, p2, q, r = (record_ref[k] for k in range(RECORD))
     w0 = mul(c0h, b0)
@@ -386,16 +388,11 @@
         run(invert_safe)
 
 
-def combine_kernel(
-    weight_ref, offset_ref, mine_ref, partner_ref, third_ref, pattern_ref, out_ref
-):
+def weights(weight_ref, offset_ref):
     _, core, _, _ = place()
     energy_count = lax.axis_size("energy")
     rank = lax.axis_index("energy")
-    half = energy_count // 2
     near = rank + 1 - 2 * (rank % 2)
-    away = 2 * rank - near
-    far = (rank + half) % energy_count
 
     def weight_of(source):
         found = jnp.float32(0.0)
@@ -404,16 +401,19 @@
         return found
 
     near_weight = weight_of(near)
-    far_weight = weight_of(far)
-    away_weight = weight_of(away)
-    mine_weight = jnp.where(core == 0, near_weight, far_weight)
-    partner_weight = jnp.where(core == 0, far_weight, near_weight)
+    far_weight = weight_of((rank + energy_count // 2) % energy_count)
+    mine = jnp.where(core == 0, near_weight, far_weight)
+    partner = jnp.where(core == 0, far_weight, near_weight)
+    return mine, partner, weight_of(2 * rank - near)
+
+
+def combine_kernel(weights_ref, mine_ref, partner_ref, third_ref, pattern_ref, out_ref):
+    mine, partner, away = (weights_ref[k, 0:1, :] for k in range(3))
     keep = pattern_ref[...].astype(F32)
     for k in range(out_ref.shape[1]):
         for part in range(2):
-            value = mine_weight * mine_ref[k, part] + partner_weight * partner_ref[k, part]
-            value = value + away_weight * third_ref[k, part]
-            out_ref[0, k, part] = value * keep
+            value = mine * mine_ref[k, part] + partner * partner_ref[k, part]
+            out_ref[0, k, part] = (value + away * third_ref[k, part]) * keep
 
 
 def kernel(body, shapes, where, scratch=(), aliases=None, result="v"):
@@ -489,7 +489,9 @@
     record, schur, corner = state
 
     message = chip_move(corner, [(middle - 1, middle), (middle, middle - 1)])
-    spread = kernel(spread_kernel, [(9,) + row], "vv")(links, record)
+    spread, shares = kernel(spread_kernel, [(9,) + row, (3, 8, n)], "ssvv")(
+        mode_weight, mode_offset, links, record
+    )
     for d in range(middle - 2, -1, -1):
         outward = [(c + 1, c) for c in range(middle - 1)] + [(c, c + 1) for c in range(middle, chips - 1)]
         fresh = backward(blocks, links, head_outward(links, message))
@@ -507,9 +509,7 @@
                 pairs.append(((2 * c + k) * energies + site, (2 * c + k) * energies + e))
     third = lax.ppermute(mine, ("space", "energy"), pairs)
     partner = lax.ppermute(theirs, "space", swap)
-    return kernel(
-        combine_kernel, [(1,) + pair], "ssvvvv", result="a"
-    )(mode_weight, mode_offset, mine, partner, third, pattern)
+    return kernel(combine_kernel, [(1,) + pair], "vvvvv", result="a")(shares, mine, partner, third, pattern)
 
 
 def solution(mesh):

time: 41 us -> 39.4 us (0.961)
  starting transfers between devices: 6.95 us -> 6.32 us
  waiting for transfers between devices: 9.35 us -> 8.77 us
    ppermute x1, starting transfers between devices: 4.54 us -> 3.64 us  [on_device(): third = lax.ppermute(mine, ('space', 'energy'), pairs)]
    pallas_call x6, Pallas kernels: 24.4 us -> 24 us  [placed(): call(*(pltpu.with_memory_space_constraint(x, spaces[w]) if w in 'vh' else...]
  transfers between devices with their start and end apart: 5 -> 5, of which waited for: 3 -> 3; matrix products, arithmetic and copies ran while one was open for 0% -> 0% of each run, Pallas kernels for 7% -> 9%
where the time goes in v4:
time: 39.4 us; the launch traced here: 39.1 us
  Pallas kernels  24 us (61%)
  waiting for transfers between devices  8.77 us (22%)
  starting transfers between devices  6.32 us (16%)
    pallas_call x6, Pallas kernels, placed(): call(*(pltpu.with_memory_space_constraint(x, spaces[w]) if w in 'vh' else...  24 us
    ppermute x1, waiting for transfers between devices, on_device(): third = lax.ppermute(mine, ('space', 'energy'), pairs)  6.19 us
    ppermute x1, starting transfers between devices, on_device(): third = lax.ppermute(mine, ('space', 'energy'), pairs)  3.64 us
    ppermute x1, waiting for transfers between devices, chip_move(): lax.ppermute(value, 'space', [(2 * a + k, 2 * b + k) for a, b in pairs fo...  2.18 us
    ppermute x1, starting transfers between devices, chip_move(): lax.ppermute(value, 'space', [(2 * a + k, 2 * b + k) for a, b in pairs fo...  1.99 us
  transfers between devices with their start and end apart: 5, of which 3 were waited for; matrix products, arithmetic and copies ran while one was open for 0% of the time, Pallas kernels for 9%

profile of v4, /device:TPU:0, one launch (start us, length us, event | category | flops | bytes accessed | tf_op | source)
XLA Modules:
  0.0 39.1 jit_solution(7960925867931148378)
XLA Ops:
  0.0 0.5 %collective-permute-start = (f32[2,2,128,128]{3,2,1,0:T(8,128)}, f32[2,2,128,128]{3,2,1,0:T(8,128)S(1)}, u32[]{:S(2)}, u32[]{:S(2)}) collective-permute-start(f32[2,2,128,128]{3,2,1,0:T(8,128)} %ham_hbm.1), channel_id=1, source_target_pairs={{0,8},{8,0},{16,24},{24,16},{1,9},{9,1},{17,25},{25,17},{2,10},{10... | collective-permute-start | bytes 786440 | tf_op jit(solution)/shard_map/ppermute | solution.py:463
  0.5 0.0 collective-permute-start.1
  0.5 1.3 %shard_map.64 = (f32[4,128,256]{2,1,0:T(8,128)S(1)}, f32[10,128,256]{2,1,0:T(8,128)S(1)}) custom-call(f32[2,2,128,128]{3,2,1,0:T(8,128)} %ham_hbm.1, f32[2,2,128,128]{3,2,1,0:T(8,128)} %cpl_hbm.1, f32[2,128,128]{2,1,0:T(8,128)} %contact_hbm.1), custom_call_target="tpu_custom_call" | custom-call | tf_op jit(solution)/shard_map/pallas_call | solution.py:438
  1.8 0.0 collective-permute-done.ham
  1.9 0.4 collective-permute-done.1.cpl
  2.2 0.4 shard_map.65
  2.6 0.0 copy-start.1
  2.7 0.0 copy-start.2
  2.7 14.2 %shard_map.66 = (f32[8,128,256]{2,1,0:T(8,128)S(1)}, f32[128,256]{1,0:T(8,128)S(1)}, f32[128,256]{1,0:T(8,128)S(1)}) custom-call(f32[4,128,256]{2,1,0:T(8,128)S(1)} %get-tuple-element.20.blocks_ref, f32[10,128,256]{2,1,0:T(8,128)S(1)} %get-tuple-element.19.links_ref, f32[128,256]{1,0:T(8,128)S(1)} %get-tuple-element.21.head_ref), custom_call_target="tpu_custom_call" | custom-call | tf_op jit(solution)/shard_map/pallas_call | solution.py:438
  16.9 2.0 %collective-permute-start.2 = (f32[128,256]{1,0:T(8,128)S(1)}, f32[128,256]{1,0:T(8,128)S(1)}, u32[]{:S(2)}, u32[]{:S(2)}) collective-permute-start(f32[128,256]{1,0:T(8,128)S(1)} %get-tuple-element.26), channel_id=1, source_target_pairs={{0,16},{8,24},{16,0},{24,8},{1,17},{9,25},{17,1},{25,9},{2,18},{10... | collective-permute-start | bytes 393224 | tf_op jit(solution)/shard_map/ppermute | solution.py:478
  18.8 0.0 copy-done.1
  18.8 0.0 copy-done.2
  18.9 2.2 %shard_map.67 = (f32[9,128,256]{2,1,0:T(8,128)S(1)}, f32[3,8,128]{2,1,0:T(8,128)S(1)}) custom-call(f32[4]{0:T(128)S(1)} %copy-done.1, s32[4]{0:T(128)S(1)} %copy-done.2, f32[10,128,256]{2,1,0:T(8,128)S(1)} %get-tuple-element.19.links_ref, f32[8,128,256]{2,1,0:T(8,128)S(1)} %get-tuple-element.22.record_ref), custom_call_target="tpu_custom_call" | custom-call | tf_op jit(solution)/shard_map/pallas_call | solution.py:438
  21.1 2.2 %collective-permute-done.2.message_ref = f32[128,256]{1,0:T(8,128)S(1)} collective-permute-done((f32[128,256]{1,0:T(8,128)S(1)}, f32[128,256]{1,0:T(8,128)S(1)}, u32[]{:S(2)}, u32[]{:S(2)}) %collective-permute-start.2) | collective-permute-done | bytes 131104 | tf_op jit(solution)/shard_map/ppermute | solution.py:478
  23.3 0.0 copy-start
  23.3 5.1 %shard_map.68 = (f32[2,2,128,128]{3,2,1,0:T(8,128)S(1)}, f32[2,2,128,128]{3,2,1,0:T(8,128)S(1)}) custom-call(f32[128,256]{1,0:T(8,128)S(1)} %get-tuple-element.24.schur_ref, f32[9,128,256]{2,1,0:T(8,128)S(1)} %get-tuple-element.25.spread_ref, f32[10,128,256]{2,1,0:T(8,128)S(1)} %get-tuple-element.19.links_ref, f32[128,256]{1,0:T(8,128)S(1)} %collective-permute-done.2.message_ref), custom_call_target="tpu_custom_call" | custom-call | tf_op jit(solution)/shard_map/pallas_call | solution.py:438
  28.4 0.2 collective-permute-start.3
  28.5 3.6 %collective-permute-start.4 = (f32[2,2,128,128]{3,2,1,0:T(8,128)S(1)}, f32[2,2,128,128]{3,2,1,0:T(8,128)S(1)}, u32[]{:S(2)}, u32[]{:S(2)}) collective-permute-start(f32[2,2,128,128]{3,2,1,0:T(8,128)S(1)} %get-tuple-element.27.mine_ref), channel_id=1, source_target_pairs={{3,1},{14,9},{0,2},{13,10},{5,3},{8,11},{2,4},{15,12},{7,5},{10,13... | collective-permute-start | bytes 786440 | tf_op jit(solution)/shard_map/ppermute | solution.py:510
  32.2 0.0 collective-permute-done.3.partner_ref
  32.2 6.2 %collective-permute-done.4.third_ref = f32[2,2,128,128]{3,2,1,0:T(8,128)S(1)} collective-permute-done((f32[2,2,128,128]{3,2,1,0:T(8,128)S(1)}, f32[2,2,128,128]{3,2,1,0:T(8,128)S(1)}, u32[]{:S(2)}, u32[]{:S(2)}) %collective-permute-start.4) | collective-permute-done | bytes 262176 | tf_op jit(solution)/shard_map/ppermute | solution.py:510
  38.4 0.0 copy-done
  38.4 0.8 %shard_map.69 = f32[1,2,2,128,128]{4,3,2,1,0:T(8,128)} custom-call(f32[3,8,128]{2,1,0:T(8,128)S(1)} %get-tuple-element.23.weights_ref, f32[2,2,128,128]{3,2,1,0:T(8,128)S(1)} %get-tuple-element.27.mine_ref, f32[2,2,128,128]{3,2,1,0:T(8,128)S(1)} %collective-permute-done.3.partner_ref, f32[2,2,128,128]{3,2,1,0:T(8,128)S(1)} %collective-permute-done.4.third_ref, ...), custom_call_target="tpu_custom_call" | custom-call | tf_op jit(solution)/shard_map/pallas_call | solution.py:438
Async XLA Ops:
  0.0 1.9 %collective-permute-start = (f32[2,2,128,128]{3,2,1,0:T(8,128)}, f32[2,2,128,128]{3,2,1,0:T(8,128)S(1)}, u32[]{:S(2)}, u32[]{:S(2)}) collective-permute-start(f32[2,2,128,128]{3,2,1,0:T(8,128)} %ham_hbm.1), channel_id=1, source_target_pairs={{0,8},{8,0},{16,24},{24,16},{1,9},{9,1},{17,25},{25,17},{2,10},{10... | collective-permute-start | bytes 786440 | tf_op jit(solution)/shard_map/ppermute | solution.py:463
  0.5 1.7 %collective-permute-start.1 = (f32[2,2,128,128]{3,2,1,0:T(8,128)}, f32[2,2,128,128]{3,2,1,0:T(8,128)S(1)}, u32[]{:S(2)}, u32[]{:S(2)}) collective-permute-start(f32[2,2,128,128]{3,2,1,0:T(8,128)} %cpl_hbm.1), channel_id=1, source_target_pairs={{0,8},{8,0},{16,24},{24,16},{1,9},{9,1},{17,25},{25,17},{2,10},{10... | collective-permute-start | bytes 786440 | tf_op jit(solution)/shard_map/ppermute | solution.py:464
  2.6 16.2 %copy-start.1 = (f32[4]{0:T(128)S(1)}, f32[4]{0:T(128)}, u32[]{:S(2)}) copy-start(f32[4]{0:T(128)} %weight_ref.1) | copy-start | bytes 52
  2.7 16.2 %copy-start.2 = (s32[4]{0:T(128)S(1)}, s32[4]{0:T(128)}, u32[]{:S(2)}) copy-start(s32[4]{0:T(128)} %offset_ref.1) | copy-start | bytes 52
  16.9 6.4 %collective-permute-start.2 = (f32[128,256]{1,0:T(8,128)S(1)}, f32[128,256]{1,0:T(8,128)S(1)}, u32[]{:S(2)}, u32[]{:S(2)}) collective-permute-start(f32[128,256]{1,0:T(8,128)S(1)} %get-tuple-element.26), channel_id=1, source_target_pairs={{0,16},{8,24},{16,0},{24,8},{1,17},{9,25},{17,1},{25,9},{2,18},{10... | collective-permute-start | bytes 393224 | tf_op jit(solution)/shard_map/ppermute | solution.py:478
  23.3 15.1 %copy-start = (s32[128,128]{1,0:T(8,128)S(1)}, s32[128,128]{1,0:T(8,128)}, u32[]{:S(2)}) copy-start(s32[128,128]{1,0:T(8,128)} %pattern_ref.1) | copy-start | bytes 196612
  28.4 3.8 %collective-permute-start.3 = (f32[2,2,128,128]{3,2,1,0:T(8,128)S(1)}, f32[2,2,128,128]{3,2,1,0:T(8,128)S(1)}, u32[]{:S(2)}, u32[]{:S(2)}) collective-permute-start(f32[2,2,128,128]{3,2,1,0:T(8,128)S(1)} %get-tuple-element.28), channel_id=1, source_target_pairs={{0,8},{8,0},{16,24},{24,16},{1,9},{9,1},{17,25},{25,17},{2,10},{10... | collective-permute-start | bytes 786440 | tf_op jit(solution)/shard_map/ppermute | solution.py:511
  28.5 9.8 %collective-permute-start.4 = (f32[2,2,128,128]{3,2,1,0:T(8,128)S(1)}, f32[2,2,128,128]{3,2,1,0:T(8,128)S(1)}, u32[]{:S(2)}, u32[]{:S(2)}) collective-permute-start(f32[2,2,128,128]{3,2,1,0:T(8,128)S(1)} %get-tuple-element.27.mine_ref), channel_id=1, source_target_pairs={{3,1},{14,9},{0,2},{13,10},{5,3},{8,11},{2,4},{15,12},{7,5},{10,13... | collective-permute-start | bytes 786440 | tf_op jit(solution)/shard_map/ppermute | solution.py:510

commit v5 on v4

--- a/solution.py
+++ b/solution.py
@@ -123,8 +123,8 @@
         n = rest.shape[0]
         c = 2.0 / (1.0 + least)
         centred = (1.0 - c) * unit(n) + c * rest
-        both = mul_low(jnp.concatenate([centred, x], 0), centred)
-        fresh.append((x + both[n:], both[:n], jnp.minimum(c * c * least, 1.0), c * gain))
+        square = mul_low(centred, centred)
+        fresh.append((x + mul_low(x, centred), square, jnp.minimum(c * c * least, 1.0), c * gain))
     return tuple(fresh)
 
 
@@ -292,7 +292,7 @@
 
     @pl.when(right == sender)
     def _():
-        corner_ref[...] = mul(mul(links_ref[BACK + end], corner_ref[...]), links_ref[end])
+        corner_ref[...] = mul_split(mul_split(links_ref[BACK + end], corner_ref[...]), links_ref[end])
 
 
 def receive(links_ref, message_ref, sigma_ref, multiplies):
@@ -301,7 +301,7 @@
 
     @pl.when(right == multiplies)
     def _():
-        sigma_ref[...] = mul(mul(links_ref[end], message_ref[...]), links_ref[BACK + end])
+        sigma_ref[...] = mul_split(mul_split(links_ref[end], message_ref[...]), links_ref[BACK + end])
 
     @pl.when(right != multiplies)
     def _():

time: 39.4 us -> 38.9 us (0.987)
  Pallas kernels: 24 us -> 23.5 us
    pallas_call x6, Pallas kernels: 24 us -> 23.5 us  [placed(): call(*(pltpu.with_memory_space_constraint(x, spaces[w]) if w in 'vh' else...]
where the time goes in v5:
time: 38.9 us; the launch traced here: 38.6 us
  Pallas kernels  23.5 us (60%)
  waiting for transfers between devices  8.62 us (22%)
  starting transfers between devices  6.45 us (17%)
    pallas_call x6, Pallas kernels, placed(): call(*(pltpu.with_memory_space_constraint(x, spaces[w]) if w in 'vh' else...  23.5 us
    ppermute x1, waiting for transfers between devices, on_device(): third = lax.ppermute(mine, ('space', 'energy'), pairs)  6.19 us
    ppermute x1, starting transfers between devices, on_device(): third = lax.ppermute(mine, ('space', 'energy'), pairs)  3.56 us
    ppermute x1, starting transfers between devices, chip_move(): lax.ppermute(value, 'space', [(2 * a + k, 2 * b + k) for a, b in pairs fo...  2.19 us
    ppermute x1, waiting for transfers between devices, chip_move(): lax.ppermute(value, 'space', [(2 * a + k, 2 * b + k) for a, b in pairs fo...  2.03 us
  transfers between devices with their start and end apart: 5, of which 3 were waited for; matrix products, arithmetic and copies ran while one was open for 0% of the time, Pallas kernels for 9%

profile of v5, /device:TPU:0, one launch (start us, length us, event | category | flops | bytes accessed | tf_op | source)
XLA Modules:
  0.0 38.6 jit_solution(11099617294190609807)
XLA Ops:
  0.0 0.5 %collective-permute-start = (f32[2,2,128,128]{3,2,1,0:T(8,128)}, f32[2,2,128,128]{3,2,1,0:T(8,128)S(1)}, u32[]{:S(2)}, u32[]{:S(2)}) collective-permute-start(f32[2,2,128,128]{3,2,1,0:T(8,128)} %ham_hbm.1), channel_id=1, source_target_pairs={{0,8},{8,0},{16,24},{24,16},{1,9},{9,1},{17,25},{25,17},{2,10},{10... | collective-permute-start | bytes 786440 | tf_op jit(solution)/shard_map/ppermute | solution.py:463
  0.5 0.0 collective-permute-start.1
  0.5 1.3 %shard_map.64 = (f32[4,128,256]{2,1,0:T(8,128)S(1)}, f32[10,128,256]{2,1,0:T(8,128)S(1)}) custom-call(f32[2,2,128,128]{3,2,1,0:T(8,128)} %ham_hbm.1, f32[2,2,128,128]{3,2,1,0:T(8,128)} %cpl_hbm.1, f32[2,128,128]{2,1,0:T(8,128)} %contact_hbm.1), custom_call_target="tpu_custom_call" | custom-call | tf_op jit(solution)/shard_map/pallas_call | solution.py:438
  1.8 0.0 collective-permute-done.ham
  1.9 0.4 collective-permute-done.1.cpl
  2.2 0.4 %shard_map.65 = (f32[4,128,256]{2,1,0:T(8,128)S(1)}, f32[10,128,256]{2,1,0:T(8,128)S(1)}, f32[128,256]{1,0:T(8,128)S(1)}) custom-call(f32[4,128,256]{2,1,0:T(8,128)S(1)} %get-tuple-element.17.own_blocks, f32[10,128,256]{2,1,0:T(8,128)S(1)} %get-tuple-element.18.own_links, ...), custom_call_target="tpu_custom_call", output_to_operand_aliasing={{0}: (0, {}), {1}: (1, {})} | custom-call | tf_op jit(solution)/shard_map/pallas_call | solution.py:438
  2.6 0.0 copy-start.1
  2.7 0.0 copy-start.2
  2.7 13.9 %shard_map.66 = (f32[8,128,256]{2,1,0:T(8,128)S(1)}, f32[128,256]{1,0:T(8,128)S(1)}, f32[128,256]{1,0:T(8,128)S(1)}) custom-call(f32[4,128,256]{2,1,0:T(8,128)S(1)} %get-tuple-element.20.blocks_ref, f32[10,128,256]{2,1,0:T(8,128)S(1)} %get-tuple-element.19.links_ref, f32[128,256]{1,0:T(8,128)S(1)} %get-tuple-element.21.head_ref), custom_call_target="tpu_custom_call" | custom-call | tf_op jit(solution)/shard_map/pallas_call | solution.py:438
  16.6 2.2 %collective-permute-start.2 = (f32[128,256]{1,0:T(8,128)S(1)}, f32[128,256]{1,0:T(8,128)S(1)}, u32[]{:S(2)}, u32[]{:S(2)}) collective-permute-start(f32[128,256]{1,0:T(8,128)S(1)} %get-tuple-element.26), channel_id=1, source_target_pairs={{0,16},{8,24},{16,0},{24,8},{1,17},{9,25},{17,1},{25,9},{2,18},{10... | collective-permute-start | bytes 393224 | tf_op jit(solution)/shard_map/ppermute | solution.py:478
  18.8 0.0 copy-done.1
  18.8 0.0 copy-done.2
  18.8 2.2 %shard_map.67 = (f32[9,128,256]{2,1,0:T(8,128)S(1)}, f32[3,8,128]{2,1,0:T(8,128)S(1)}) custom-call(f32[4]{0:T(128)S(1)} %copy-done.1, s32[4]{0:T(128)S(1)} %copy-done.2, f32[10,128,256]{2,1,0:T(8,128)S(1)} %get-tuple-element.19.links_ref, f32[8,128,256]{2,1,0:T(8,128)S(1)} %get-tuple-element.22.record_ref), custom_call_target="tpu_custom_call" | custom-call | tf_op jit(solution)/shard_map/pallas_call | solution.py:438
  21.0 2.0 %collective-permute-done.2.message_ref = f32[128,256]{1,0:T(8,128)S(1)} collective-permute-done((f32[128,256]{1,0:T(8,128)S(1)}, f32[128,256]{1,0:T(8,128)S(1)}, u32[]{:S(2)}, u32[]{:S(2)}) %collective-permute-start.2) | collective-permute-done | bytes 131104 | tf_op jit(solution)/shard_map/ppermute | solution.py:478
  23.1 0.0 copy-start
  23.1 4.8 %shard_map.68 = (f32[2,2,128,128]{3,2,1,0:T(8,128)S(1)}, f32[2,2,128,128]{3,2,1,0:T(8,128)S(1)}) custom-call(f32[128,256]{1,0:T(8,128)S(1)} %get-tuple-element.24.schur_ref, f32[9,128,256]{2,1,0:T(8,128)S(1)} %get-tuple-element.25.spread_ref, f32[10,128,256]{2,1,0:T(8,128)S(1)} %get-tuple-element.19.links_ref, f32[128,256]{1,0:T(8,128)S(1)} %collective-permute-done.2.message_ref), custom_call_target="tpu_custom_call" | custom-call | tf_op jit(solution)/shard_map/pallas_call | solution.py:438
  27.9 0.2 collective-permute-start.3
  28.1 3.6 %collective-permute-start.4 = (f32[2,2,128,128]{3,2,1,0:T(8,128)S(1)}, f32[2,2,128,128]{3,2,1,0:T(8,128)S(1)}, u32[]{:S(2)}, u32[]{:S(2)}) collective-permute-start(f32[2,2,128,128]{3,2,1,0:T(8,128)S(1)} %get-tuple-element.27.mine_ref), channel_id=1, source_target_pairs={{3,1},{14,9},{0,2},{13,10},{5,3},{8,11},{2,4},{15,12},{7,5},{10,13... | collective-permute-start | bytes 786440 | tf_op jit(solution)/shard_map/ppermute | solution.py:510
  31.7 0.0 collective-permute-done.3.partner_ref
  31.7 6.2 %collective-permute-done.4.third_ref = f32[2,2,128,128]{3,2,1,0:T(8,128)S(1)} collective-permute-done((f32[2,2,128,128]{3,2,1,0:T(8,128)S(1)}, f32[2,2,128,128]{3,2,1,0:T(8,128)S(1)}, u32[]{:S(2)}, u32[]{:S(2)}) %collective-permute-start.4) | collective-permute-done | bytes 262176 | tf_op jit(solution)/shard_map/ppermute | solution.py:510
  37.9 0.0 copy-done
  37.9 0.8 %shard_map.69 = f32[1,2,2,128,128]{4,3,2,1,0:T(8,128)} custom-call(f32[3,8,128]{2,1,0:T(8,128)S(1)} %get-tuple-element.23.weights_ref, f32[2,2,128,128]{3,2,1,0:T(8,128)S(1)} %get-tuple-element.27.mine_ref, f32[2,2,128,128]{3,2,1,0:T(8,128)S(1)} %collective-permute-done.3.partner_ref, f32[2,2,128,128]{3,2,1,0:T(8,128)S(1)} %collective-permute-done.4.third_ref, ...), custom_call_target="tpu_custom_call" | custom-call | tf_op jit(solution)/shard_map/pallas_call | solution.py:438
Async XLA Ops:
  0.0 1.9 %collective-permute-start = (f32[2,2,128,128]{3,2,1,0:T(8,128)}, f32[2,2,128,128]{3,2,1,0:T(8,128)S(1)}, u32[]{:S(2)}, u32[]{:S(2)}) collective-permute-start(f32[2,2,128,128]{3,2,1,0:T(8,128)} %ham_hbm.1), channel_id=1, source_target_pairs={{0,8},{8,0},{16,24},{24,16},{1,9},{9,1},{17,25},{25,17},{2,10},{10... | collective-permute-start | bytes 786440 | tf_op jit(solution)/shard_map/ppermute | solution.py:463
  0.5 1.7 %collective-permute-start.1 = (f32[2,2,128,128]{3,2,1,0:T(8,128)}, f32[2,2,128,128]{3,2,1,0:T(8,128)S(1)}, u32[]{:S(2)}, u32[]{:S(2)}) collective-permute-start(f32[2,2,128,128]{3,2,1,0:T(8,128)} %cpl_hbm.1), channel_id=1, source_target_pairs={{0,8},{8,0},{16,24},{24,16},{1,9},{9,1},{17,25},{25,17},{2,10},{10... | collective-permute-start | bytes 786440 | tf_op jit(solution)/shard_map/ppermute | solution.py:464
  2.6 16.2 %copy-start.1 = (f32[4]{0:T(128)S(1)}, f32[4]{0:T(128)}, u32[]{:S(2)}) copy-start(f32[4]{0:T(128)} %weight_ref.1) | copy-start | bytes 52
  2.7 16.1 %copy-start.2 = (s32[4]{0:T(128)S(1)}, s32[4]{0:T(128)}, u32[]{:S(2)}) copy-start(s32[4]{0:T(128)} %offset_ref.1) | copy-start | bytes 52
  16.6 6.5 %collective-permute-start.2 = (f32[128,256]{1,0:T(8,128)S(1)}, f32[128,256]{1,0:T(8,128)S(1)}, u32[]{:S(2)}, u32[]{:S(2)}) collective-permute-start(f32[128,256]{1,0:T(8,128)S(1)} %get-tuple-element.26), channel_id=1, source_target_pairs={{0,16},{8,24},{16,0},{24,8},{1,17},{9,25},{17,1},{25,9},{2,18},{10... | collective-permute-start | bytes 393224 | tf_op jit(solution)/shard_map/ppermute | solution.py:478
  23.1 14.8 %copy-start = (s32[128,128]{1,0:T(8,128)S(1)}, s32[128,128]{1,0:T(8,128)}, u32[]{:S(2)}) copy-start(s32[128,128]{1,0:T(8,128)} %pattern_ref.1) | copy-start | bytes 196612
  27.9 3.8 %collective-permute-start.3 = (f32[2,2,128,128]{3,2,1,0:T(8,128)S(1)}, f32[2,2,128,128]{3,2,1,0:T(8,128)S(1)}, u32[]{:S(2)}, u32[]{:S(2)}) collective-permute-start(f32[2,2,128,128]{3,2,1,0:T(8,128)S(1)} %get-tuple-element.28), channel_id=1, source_target_pairs={{0,8},{8,0},{16,24},{24,16},{1,9},{9,1},{17,25},{25,17},{2,10},{10... | collective-permute-start | bytes 786440 | tf_op jit(solution)/shard_map/ppermute | solution.py:511
  28.1 9.8 %collective-permute-start.4 = (f32[2,2,128,128]{3,2,1,0:T(8,128)S(1)}, f32[2,2,128,128]{3,2,1,0:T(8,128)S(1)}, u32[]{:S(2)}, u32[]{:S(2)}) collective-permute-start(f32[2,2,128,128]{3,2,1,0:T(8,128)S(1)} %get-tuple-element.27.mine_ref), channel_id=1, source_target_pairs={{3,1},{14,9},{0,2},{13,10},{5,3},{8,11},{2,4},{15,12},{7,5},{10,13... | collective-permute-start | bytes 786440 | tf_op jit(solution)/shard_map/ppermute | solution.py:510
